TPU v7x, 32 devices: a whole 2x2x4 slice. The times are simulated.
32 devices in a mesh: dp: 16 (over z, x, core), seq: 2 (over y).
Axes of the slice: x: 2, y: 2, z: 4, core: 2. Of those that a mesh axis runs over, the one named last changes fastest.
Arguments:
- hidden_in: bfloat16 [32, 1024, 1024], P('dp', 'seq'), may hold values from -6 to 6
- family: int32 [16], P('dp'), may hold values from 0 to 63
- orient: int32 [32], P('dp'), may hold values from 0 to 1, as said below
- norm_gain: bfloat16 [1024], replicated, may hold values from 0.099609375 to 1.8984375
- norm_bias: bfloat16 [1024], replicated, may hold values from -4 to 4
- qkv_weight: bfloat16 [1024, 3072], replicated, may hold values from -0.1875 to 0.1875
- out_weight: bfloat16 [1024, 1024], replicated, may hold values from -0.5 to 0.5
- up_weight: bfloat16 [1024, 4096], replicated, may hold values from -0.1875 to 0.1875
- up_bias: bfloat16 [4096], replicated, may hold values from -6 to 6
- down_weight: bfloat16 [4096, 1024], replicated, may hold values from -0.09375 to 0.09375
- down_bias: bfloat16 [1024], replicated, may hold values from -4 to 4
- family_table: bfloat16 [64, 1024], replicated, may hold values from -6 to 6
- orient_table: bfloat16 [2, 1024], replicated, may hold values from -6 to 6
- cotangent: bfloat16 [32, 1024, 1024], P('dp', 'seq'), may hold values from -6 to 6
Outputs:
- layer_out: bfloat16 [32, 1024, 1024], P('dp', 'seq')
- input_grad: float32 [32, 1024, 1024], P('dp', 'seq')
- norm_gain_grad: float32 [1024], replicated
- norm_bias_grad: float32 [1024], replicated
- qkv_weight_grad: float32 [1024, 3072], P(('dp', 'seq'))
- out_weight_grad: float32 [1024, 1024], P(('dp', 'seq'))
- up_weight_grad: float32 [1024, 4096], P(('dp', 'seq'))
- up_bias_grad: float32 [4096], replicated
- down_weight_grad: float32 [4096, 1024], P(('dp', 'seq'))
- down_bias_grad: float32 [1024], replicated
- family_table_grad: float32 [64, 1024], replicated
- orient_table_grad: float32 [2, 1024], replicated
Inputs may be any that keep to these rules, and one draw needn't show every extreme that they name: `orient`: in each pair of rows 2p and 2p + 1 one row has flag 0 and the other flag 1.
All inputs are finite; a program needn't handle non-finite values.
Results may differ from a plain program's by a relative error of at most 0.006.
Values may be sent and summed in bfloat16 or wider, within the bound.
A program may use at most 256 MiB of HBM per device.

v0:
```python
import math

import jax
import jax.numpy as jnp
from jax import lax
from jax.sharding import PartitionSpec as P

H = 16
HD = 64
ROT = 32


def for_sending(shard):

    def short(part):
        return part.astype(jnp.bfloat16) if part.dtype == jnp.float32 else part

    return jax.tree.map(short, shard)


def rope_tables(positions, features):
    column = jnp.arange(features, dtype=jnp.int32)
    within = column % HD
    frequency = jnp.exp(-(2.0 * (within // 2).astype(jnp.float32) / ROT) * math.log(10000.0))
    angles = positions[:, None] * frequency[None, :]
    rotary = within < ROT
    cosine = jnp.where(rotary[None, :], jnp.cos(angles), 1.0)
    sign_term = jnp.where(within % 2 == 0, -1.0, 1.0)
    sine_term = jnp.where(rotary[None, :], sign_term[None, :] * jnp.sin(angles), 0.0)
    return (cosine, sine_term)


def pair_swap(values):
    even_cols = jnp.arange(values.shape[-1]) % 2 == 0
    return jnp.where(even_cols, jnp.roll(values, -1, axis=-1), jnp.roll(values, 1, axis=-1))


def rotate(values, cosine, sine_term):
    return values * cosine + pair_swap(values) * sine_term


def rotate_back(values, cosine, sine_term):
    return values * cosine + pair_swap(values * sine_term)


def gelu_tanh(pre_values):
    return jax.nn.gelu(pre_values, approximate=True)


def body(
    hidden_in,
    family,
    orient,
    norm_gain,
    norm_bias,
    qkv_weight,
    out_weight,
    up_weight,
    up_bias,
    down_weight,
    down_bias,
    family_table,
    orient_table,
    cotangent,
):
    seq_count = lax.axis_size("seq")
    row_count, seg_length, features = hidden_in.shape
    full_length = seg_length * seq_count
    local_heads = H // seq_count
    head_size = features // H
    slab_width = features // seq_count
    block_rows = min(512, full_length)
    block_count = full_length // block_rows
    score_scale = head_size ** (-0.5)
    token_count = row_count * seg_length
    family_rows = jnp.repeat(family, 2)
    family_hot = (family_rows[:, None] == jnp.arange(family_table.shape[0])[None, :]).astype(
        jnp.bfloat16
    )
    orient_hot = (orient[:, None] == jnp.arange(2)[None, :]).astype(jnp.bfloat16)
    embedding = jnp.dot(family_hot, family_table, preferred_element_type=jnp.float32) + jnp.dot(
        orient_hot, orient_table, preferred_element_type=jnp.float32
    )
    embedded = (hidden_in.astype(jnp.float32) + embedding[:, None, :]).reshape(
        token_count, features
    )
    row_mean = jnp.mean(embedded, -1, keepdims=True)
    centred = embedded - row_mean
    row_var = jnp.mean(centred * centred, -1, keepdims=True)
    inv_std = lax.rsqrt(row_var + 1e-05)
    normed_hat = centred * inv_std
    gain_f32 = norm_gain.astype(jnp.float32)
    normed_low = (normed_hat * gain_f32 + norm_bias.astype(jnp.float32)).astype(jnp.bfloat16)
    projected = jnp.dot(normed_low, qkv_weight, preferred_element_type=jnp.float32).reshape(
        row_count, seg_length, 3 * features
    )
    positions = (lax.axis_index("seq") * seg_length + jnp.arange(seg_length)).astype(jnp.float32)
    cosine, sine_term = rope_tables(positions, features)
    queries = rotate(projected[..., :features], cosine, sine_term).astype(jnp.bfloat16)
    keys_rot = rotate(projected[..., features : 2 * features], cosine, sine_term).astype(
        jnp.bfloat16
    )
    values = projected[..., 2 * features :].astype(jnp.bfloat16)
    query_heads, key_heads, value_heads = (
        lax.all_to_all(queries, "seq", split_axis=2, concat_axis=1, tiled=True),
        lax.all_to_all(keys_rot, "seq", split_axis=2, concat_axis=1, tiled=True),
        lax.all_to_all(values, "seq", split_axis=2, concat_axis=1, tiled=True),
    )

    def scores_for(query_block, key_rows, block_start):
        logits = (
            jnp.einsum("qhd,khd->hqk", query_block, key_rows, preferred_element_type=jnp.float32)
            * score_scale
        )
        causal = (block_start + jnp.arange(block_rows))[:, None] >= jnp.arange(full_length)[None, :]
        return jnp.where(causal[None], logits, -1e30)

    def attend(row_args):
        query_row, key_row, value_row = row_args
        key_rows = key_row.reshape(full_length, local_heads, head_size)
        value_rows = value_row.reshape(full_length, local_heads, head_size)
        pieces = []
        log_parts = []
        for block_index in range(block_count):
            block_start = block_index * block_rows
            query_block = query_row[block_start : block_start + block_rows].reshape(
                block_rows, local_heads, head_size
            )
            logits = scores_for(query_block, key_rows, block_start)
            row_peak = jnp.max(logits, -1, keepdims=True)
            weights = jnp.exp(logits - row_peak)
            row_total = jnp.sum(weights, -1, keepdims=True)
            prob_low = (weights / row_total).astype(jnp.bfloat16)
            output_block = jnp.einsum(
                "hqk,khd->qhd", prob_low, value_rows, preferred_element_type=jnp.float32
            )
            pieces.append(output_block.reshape(block_rows, slab_width).astype(jnp.bfloat16))
            log_parts.append((row_peak + jnp.log(row_total))[..., 0])
        return (jnp.concatenate(pieces, 0), jnp.concatenate(log_parts, 1))

    attended_heads, log_sums = lax.map(attend, (query_heads, key_heads, value_heads))
    attended = jax.tree.map(
        lambda part, own: part.astype(own.dtype),
        lax.all_to_all(for_sending(attended_heads), "seq", split_axis=1, concat_axis=2, tiled=True),
        attended_heads,
    )
    attended_flat = attended.reshape(token_count, features)
    branch_attn = jnp.dot(attended_flat, out_weight, preferred_element_type=jnp.float32)
    up_pre = jnp.dot(normed_low, up_weight, preferred_element_type=jnp.float32) + up_bias.astype(
        jnp.float32
    )
    up_act = gelu_tanh(up_pre).astype(jnp.bfloat16)
    branch_feed = jnp.dot(
        up_act, down_weight, preferred_element_type=jnp.float32
    ) + down_bias.astype(jnp.float32)
    layer_out = (
        (embedded + branch_attn + branch_feed)
        .astype(jnp.bfloat16)
        .reshape(row_count, seg_length, features)
    )
    grad_low = cotangent.reshape(token_count, features)
    grad_f32 = grad_low.astype(jnp.float32)
    down_grad = jnp.einsum("nf,nd->fd", up_act, grad_low, preferred_element_type=jnp.float32)
    down_bias_grad = jnp.sum(grad_f32, 0)
    act_grad = jnp.einsum("nd,fd->nf", grad_low, down_weight, preferred_element_type=jnp.float32)
    gelu_out, gelu_pull = jax.vjp(gelu_tanh, up_pre)
    pre_grad = gelu_pull(act_grad)[0].astype(jnp.bfloat16)
    up_bias_grad = jnp.sum(pre_grad.astype(jnp.float32), 0)
    up_grad = jnp.einsum("nd,nf->df", normed_low, pre_grad, preferred_element_type=jnp.float32)
    normed_grad = jnp.einsum("nf,df->nd", pre_grad, up_weight, preferred_element_type=jnp.float32)
    out_grad = jnp.einsum("nd,ne->de", attended_flat, grad_low, preferred_element_type=jnp.float32)
    attended_grad = jnp.einsum(
        "ne,de->nd", grad_low, out_weight, preferred_element_type=jnp.float32
    )
    attended_grad = attended_grad.astype(jnp.bfloat16).reshape(row_count, seg_length, features)
    grad_heads = lax.all_to_all(attended_grad, "seq", split_axis=2, concat_axis=1, tiled=True)

    def attend_back(row_args):
        query_row, key_row, value_row, grad_row, log_row = row_args
        key_rows = key_row.reshape(full_length, local_heads, head_size)
        value_rows = value_row.reshape(full_length, local_heads, head_size)
        keys_total = jnp.zeros((full_length, local_heads, head_size), jnp.float32)
        values_total = jnp.zeros((full_length, local_heads, head_size), jnp.float32)
        query_parts = []
        for block_index in range(block_count):
            block_start = block_index * block_rows
            query_block = query_row[block_start : block_start + block_rows].reshape(
                block_rows, local_heads, head_size
            )
            grad_block = grad_row[block_start : block_start + block_rows].reshape(
                block_rows, local_heads, head_size
            )
            logits = scores_for(query_block, key_rows, block_start)
            probs_full = jnp.exp(logits - log_row[:, block_start : block_start + block_rows, None])
            prob_low = probs_full.astype(jnp.bfloat16)
            probs_grad = jnp.einsum(
                "qhd,khd->hqk", grad_block, value_rows, preferred_element_type=jnp.float32
            )
            inner_sum = jnp.sum(probs_full * probs_grad, -1, keepdims=True)
            scores_grad = (probs_full * (probs_grad - inner_sum)).astype(jnp.bfloat16)
            values_total = values_total + jnp.einsum(
                "hqk,qhd->khd", prob_low, grad_block, preferred_element_type=jnp.float32
            )
            query_grad = (
                jnp.einsum(
                    "hqk,khd->qhd", scores_grad, key_rows, preferred_element_type=jnp.float32
                )
                * score_scale
            )
            query_parts.append(query_grad.reshape(block_rows, slab_width).astype(jnp.bfloat16))
            keys_total = (
                keys_total
                + jnp.einsum(
                    "hqk,qhd->khd", scores_grad, query_block, preferred_element_type=jnp.float32
                )
                * score_scale
            )
        return (
            jnp.concatenate(query_parts, 0),
            keys_total.reshape(full_length, slab_width).astype(jnp.bfloat16),
            values_total.reshape(full_length, slab_width).astype(jnp.bfloat16),
        )

    query_grad_heads, key_grad_heads, value_grad_heads = lax.map(
        attend_back, (query_heads, key_heads, value_heads, grad_heads, log_sums)
    )
    query_grad_pos, key_grad_pos, value_grad_pos = (
        lax.all_to_all(
            for_sending(query_grad_heads), "seq", split_axis=1, concat_axis=2, tiled=True
        ).astype(query_grad_heads.dtype),
        lax.all_to_all(
            for_sending(key_grad_heads), "seq", split_axis=1, concat_axis=2, tiled=True
        ).astype(key_grad_heads.dtype),
        lax.all_to_all(
            for_sending(value_grad_heads), "seq", split_axis=1, concat_axis=2, tiled=True
        ).astype(value_grad_heads.dtype),
    )
    projected_grad = jnp.concatenate(
        [
            rotate_back(query_grad_pos.astype(jnp.float32), cosine, sine_term),
            rotate_back(key_grad_pos.astype(jnp.float32), cosine, sine_term),
            value_grad_pos.astype(jnp.float32),
        ],
        -1,
    )
    projected_grad = projected_grad.astype(jnp.bfloat16).reshape(token_count, 3 * features)
    qkv_grad = jnp.einsum(
        "nd,ne->de", normed_low, projected_grad, preferred_element_type=jnp.float32
    )
    normed_grad = normed_grad + jnp.einsum(
        "ne,de->nd", projected_grad, qkv_weight, preferred_element_type=jnp.float32
    )
    gain_grad = jnp.sum(normed_grad * normed_hat, 0)
    bias_grad = jnp.sum(normed_grad, 0)
    scaled_grad = normed_grad * gain_f32
    hat_grad = (
        scaled_grad
        - jnp.mean(scaled_grad, -1, keepdims=True)
        - normed_hat * jnp.mean(scaled_grad * normed_hat, -1, keepdims=True)
    )
    input_grad = (grad_f32 + inv_std * hat_grad).reshape(row_count, seg_length, features)
    row_sums = jnp.sum(input_grad, 1)
    family_grad = jnp.einsum(
        "rf,rd->fd", family_hot.astype(jnp.float32), row_sums, precision=lax.Precision.HIGHEST
    )
    orient_grad = jnp.einsum(
        "rf,rd->fd", orient_hot.astype(jnp.float32), row_sums, precision=lax.Precision.HIGHEST
    )
    gain_sum, bias_sum, up_bias_sum, down_bias_sum, family_sum, orient_sum = lax.psum(
        (gain_grad, bias_grad, up_bias_grad, down_bias_grad, family_grad, orient_grad),
        ("dp", "seq"),
    )
    qkv_sum, out_sum, up_sum, down_sum = (
        lax.psum_scatter(qkv_grad, ("dp", "seq"), scatter_dimension=0, tiled=True),
        lax.psum_scatter(out_grad, ("dp", "seq"), scatter_dimension=0, tiled=True),
        lax.psum_scatter(up_grad, ("dp", "seq"), scatter_dimension=0, tiled=True),
        lax.psum_scatter(down_grad, ("dp", "seq"), scatter_dimension=0, tiled=True),
    )
    return (
        layer_out,
        input_grad,
        gain_sum,
        bias_sum,
        qkv_sum,
        out_sum,
        up_sum,
        up_bias_sum,
        down_sum,
        down_bias_sum,
        family_sum,
        orient_sum,
    )


def solution(mesh):
    return jax.shard_map(
        body,
        mesh=mesh,
        in_specs=(
            P("dp", "seq", None),
            P("dp"),
            P("dp"),
            P(),
            P(),
            P(),
            P(),
            P(),
            P(),
            P(),
            P(),
            P(),
            P(),
            P("dp", "seq", None),
        ),
        out_specs=(
            P("dp", "seq", None),
            P("dp", "seq", None),
            P(),
            P(),
            P(("dp", "seq"), None),
            P(("dp", "seq"), None),
            P(("dp", "seq"), None),
            P(),
            P(("dp", "seq"), None),
            P(),
            P(),
            P(),
        ),
        check_vma=False,
    )
```

profile of v0, /device:TPU:0, one launch (start us, length us, event | category | flops | bytes accessed | tf_op | source)
XLA Modules:
  0.0 1835.0 jit_solution(17062700725585724504)
XLA Ops:
  15.1 7.0 fusion.30
  22.1 7.6 fusion.89
  33.1 7.5 fusion.48
  40.6 12.5 fusion.37
  53.2 6.2 copy.51
  64.6 6.2 copy.53
  70.8 20.2 %all-to-all-done.1 = bf16[2,512,1024]{1,0,2:T(2,128)(2,1)} async-done(((bf16[2,512,1024]{1,0,2:T(2,128)(2,1)}), bf16[2,512,1024]{1,0,2:T(2,128)(2,1)}, u32[]{:S(2)}, u32[]{:S(2)}) %all-to-all-start.1) | async-done | bytes 2097184 | tf_op jit(solution)/shard_map/all_to_all | solution.py:105
  99.6 6.2 copy.49
  105.8 14.6 all-to-all-done.2
  125.3 5.3 convolution_convert_fusion
  130.6 6.2 copy.57
  176.7 84.7 %while.26 = (s32[]{:T(128)}, bf16[2,1024,512]{1,2,0:T(8,128)(2,1)}, f32[2,8,1024]{2,1,0:T(8,128)S(1)}, bf16[2,1024,512]{1,2,0:T(8,128)(2,1)}, bf16[2,1024,512]{1...) while((s32[]{:T(128)}, bf16[2,1024,512]{1,2,0:T(8,128)(2,1)}, ...), condition=%wide.region_7.8_spmd, body=%wide.region_2.7_spmd.sunk | while | flops 2251817472 | bytes 124064400 | solution.py:141
  188.6 7.4 fusion.195
  196.0 8.1 fusion.196
  204.2 5.6 fusion.200
  209.8 8.2 fusion.197
  231.0 7.4 fusion.195
  238.4 8.1 fusion.196
  246.5 5.6 fusion.200
  252.1 8.2 fusion.197
  275.8 202.6 %while.27 = (s32[]{:T(128)}, bf16[2,1024,512]{1,2,0:T(8,128)(2,1)}, bf16[2,1024,512]{1,2,0:T(8,128)(2,1)}, bf16[2,1024,512]{1,2,0:T(8,128)(2,1)}, bf16[2,1024,51...) while((s32[]{:T(128)}, bf16[2,1024,512]{1,2,0:T(8,128)(2,1)}, ...), condition=%wide.region_11.12_spmd, body=%wide.region_8.11_spmd.sunk | while | flops 5451014656 | bytes 458462208 | solution.py:224
  278.8 8.1 fusion.226
  287.3 12.6 multiply_reduce_fusion.9
  300.0 11.3 multiply_convert_fusion.10
  314.6 8.1 fusion.223
  323.1 12.6 multiply_reduce_fusion.8
  335.7 11.3 multiply_convert_fusion.9
  352.4 6.6 fusion.227
  359.0 7.5 fusion.228
  368.1 6.2 fusion.225
  379.8 8.1 fusion.226
  388.4 12.6 multiply_reduce_fusion.9
  401.0 11.3 multiply_convert_fusion.10
  415.6 8.1 fusion.223
  424.1 12.6 multiply_reduce_fusion.8
  436.7 11.3 multiply_convert_fusion.9
  453.4 6.5 fusion.227
  460.0 7.5 fusion.228
  469.1 6.2 fusion.225
  478.4 6.2 copy.59
  489.4 16.0 fusion.98
  505.4 6.2 copy.63
  517.9 26.5 %convert_reduce_fusion = (f32[4096]{0:T(1024)}, bf16[1024,4096]{1,0:T(8,128)(2,1)}) fusion(f32[1024,4096]{1,0:T(8,128)} %fusion.98, f32[4096]{0:T(1024)S(1)} %copy-done.35, bf16[1024,1024]{1,0:T(8,128)(2,1)} %bitcast.316, bf16[4096,1024]{1,0:T(8,128)(2,1)} %param.27), kind=kOutput, calls=%fused_computation.70 | convolution fusion | flops 8686399488 | bytes 35684352 | tf_op jit(solution)/shard_map/nd,fd->nf/dot_general | solution.py:165
  544.4 6.2 copy.67
  550.5 6.4 copy.55
  556.9 5.8 copy.78
  562.7 5.8 copy.60
  573.3 5.8 copy.77
  579.1 5.7 copy.64
  584.8 7.0 reshape.472
  591.8 6.7 reshape.474
  598.5 5.4 broadcast_multiply_fusion.1
  633.0 9.3 fusion.33
  642.3 13.1 fusion.46
  655.5 15.7 multiply_reduce_fusion.2
  687.5 12.8 fusion.45
  700.8 16.2 fusion.100
  717.1 20.2 %fusion.85 = f32[4096,1024]{1,0:T(8,128)} fusion(bf16[1024,1024]{1,0:T(8,128)(2,1)} %bitcast.317, f32[1024,4096]{1,0:T(8,128)} %fusion.98, f32[4096]{0:T(1024)S(1)} %copy-done.35), kind=kOutput, calls=%fused_computation.174 | convolution fusion | flops 8631877632 | bytes 35667968 | tf_op jit(solution)/shard_map/nf,nd->fd/dot_general | solution.py:163
  740.2 41.9 %all-reduce = (f32[1024]{0:T(1024)}, f32[1024]{0:T(1024)}, f32[4096]{0:T(1024)}, f32[1024]{0:T(1024)}, f32[2,1024]{1,0:T(2,128)}) all-reduce(f32[1024]{0:T(1024)S(1)} %get-tuple-element.99, f32[1024]{0:T(1024)S(1)} %get-tuple-element.102, f32[4096]{0:T(1024)S(1)} %copy-done.36, ...), channel_id=1, replica_groups=mesh['dp'=16,'seq'=2] {'dp','seq'}, use_global_device_ids=true, to_apply=%region_15.16 | all-reduce | flops 9216 | bytes 73728 | tf_op jit(solution)/shard_map/psum | solution.py:269
  786.2 17.8 fusion.43
  804.0 142.8 %reduce-scatter.7.cloned.1.call-done = f32[32,1024]{1,0:T(8,128)} async-done(((f32[1024,1024]{1,0:T(8,128)}), f32[32,1024]{1,0:T(8,128)}) %reduce-scatter.7.cloned.1.call-update) | async-done | bytes 131088 | tf_op jit(solution)/shard_map/reduce_scatter | solution.py:275
  946.8 159.1 %reduce-scatter.5.cloned.1.call-done = f32[32,3072]{1,0:T(8,128)} async-done(((f32[1024,3072]{1,0:T(8,128)}), f32[32,3072]{1,0:T(8,128)}) %reduce-scatter.5.cloned.1.call-update) | async-done | bytes 393232 | tf_op jit(solution)/shard_map/reduce_scatter | solution.py:274
  1105.9 359.3 %reduce-scatter.9.cloned.1.call-done = f32[32,4096]{1,0:T(8,128)} async-done(((f32[1024,4096]{1,0:T(8,128)}), f32[32,4096]{1,0:T(8,128)}) %reduce-scatter.9.cloned.1.call-update) | async-done | bytes 524304 | tf_op jit(solution)/shard_map/reduce_scatter | solution.py:276
  1465.3 361.3 %reduce-scatter.11.cloned.1.call-done = f32[128,1024]{1,0:T(8,128)} async-done(((f32[4096,1024]{1,0:T(8,128)}), f32[128,1024]{1,0:T(8,128)}) %reduce-scatter.11.cloned.1.call-update) | async-done | bytes 524304 | tf_op jit(solution)/shard_map/reduce_scatter | solution.py:277
  (258 shorter events, 212.5 us)
Async XLA Ops:
  7.2 118.1 %copy-start = (bf16[1024,1024]{1,0:T(8,128)(2,1)S(1)}, bf16[1024,1024]{1,0:T(8,128)(2,1)}, u32[]{:S(2)}) copy-start(bf16[1024,1024]{1,0:T(8,128)(2,1)} %param.24) | copy-start | bytes 6291460
  7.2 7.0 copy-start.19
  10.1 5.0 copy-start.42
  10.1 5.0 copy-start.43
  10.1 5.0 copy-start.45
  15.1 122.3 %copy-start.29 = (f32[1024]{0:T(1024)}, f32[1024]{0:T(1024)S(1)}, u32[]{:S(2)}) copy-start(f32[1024]{0:T(1024)S(1)} %convert_element_type.207) | copy-start | bytes 12292
  22.0 9.6 copy-start.5
  33.0 20.2 %copy-start.38 = (pred[1024]{0:T(1024)(128)(4,1)}, pred[1024]{0:T(1024)(128)(4,1)S(1)}, u32[]{:S(2)}) copy-start(pred[1024]{0:T(1024)(128)(4,1)S(1)} %fusion.61) | copy-start | bytes 3076
  33.0 7.6 copy-start.16
  40.6 12.6 copy-start.9
  40.6 12.6 copy-start.11
  59.3 31.6 %all-to-all-start.1 = ((bf16[2,512,1024]{1,0,2:T(2,128)(2,1)}), bf16[2,512,1024]{1,0,2:T(2,128)(2,1)}, u32[]{:S(2)}, u32[]{:S(2)}) async-start(bf16[2,512,1024]{1,0,2:T(2,128)(2,1)} %copy.51), calls=%async_computation.1 | async-start | bytes 4194304 | tf_op jit(solution)/shard_map/all_to_all | solution.py:105
  91.0 29.4 %all-to-all-start.2 = ((bf16[2,512,1024]{1,0,2:T(2,128)(2,1)}), bf16[2,512,1024]{1,0,2:T(2,128)(2,1)}, u32[]{:S(2)}, u32[]{:S(2)}) async-start(bf16[2,512,1024]{1,0,2:T(2,128)(2,1)} %copy.53), calls=%async_computation.2 | async-start | bytes 4194304 | tf_op jit(solution)/shard_map/all_to_all | solution.py:106
  120.4 40.2 %all-to-all-start = ((bf16[2,512,1024]{1,0,2:T(2,128)(2,1)}), bf16[2,512,1024]{1,0,2:T(2,128)(2,1)}, u32[]{:S(2)}, u32[]{:S(2)}) async-start(bf16[2,512,1024]{1,0,2:T(2,128)(2,1)} %copy.49), calls=%async_computation | async-start | bytes 4194304 | tf_op jit(solution)/shard_map/all_to_all | solution.py:107
  130.6 6.2 copy-start.37
  136.7 4.9 copy-start.31
  136.7 4.9 copy-start.33
  160.6 100.8 %all-to-all-start.4 = ((bf16[2,512,1024]{1,0,2:T(2,128)(2,1)}), bf16[2,512,1024]{1,0,2:T(2,128)(2,1)}, u32[]{:S(2)}, u32[]{:S(2)}) async-start(bf16[2,512,1024]{1,0,2:T(2,128)(2,1)} %copy.57), calls=%async_computation.4 | async-start | bytes 4194304 | tf_op jit(solution)/shard_map/all_to_all | solution.py:176
  196.0 8.1 copy-start.8
  238.4 8.1 copy-start.8
  278.8 8.2 copy-start.4
  278.8 8.3 copy-start.3
  311.3 3.3 copy-start.2
  347.0 4.3 copy-start.1
  347.1 19.4 %slice-start = ((s8[16777216]{0:T(1024)(128)(4,1)}), s8[4194304]{0:T(1024)(128)(4,1)S(1)}, s32[]{:S(2)}) async-start(s8[16777216]{0:T(1024)(128)(4,1)} %bitcast.276), calls=%async_computation.17 | async-start | bytes 8388608 | tf_op jit(solution)/shard_map/while
  347.1 19.4 %slice-start.1 = ((s8[16777216]{0:T(1024)(128)(4,1)}), s8[4194304]{0:T(1024)(128)(4,1)S(1)}, s32[]{:S(2)}) async-start(s8[16777216]{0:T(1024)(128)(4,1)} %bitcast.276), calls=%async_computation.18 | async-start | bytes 8388608 | tf_op jit(solution)/shard_map/while
  352.4 14.1 slice-start.2
  359.0 7.5 slice-start.3
  368.1 6.2 copy-start.20
  368.1 6.2 copy-start.22
  379.8 8.2 copy-start.4
  379.8 8.3 copy-start.3
  412.3 3.3 copy-start.2
  448.0 4.3 copy-start.1
  448.1 19.4 %slice-start = ((s8[16777216]{0:T(1024)(128)(4,1)}), s8[4194304]{0:T(1024)(128)(4,1)S(1)}, s32[]{:S(2)}) async-start(s8[16777216]{0:T(1024)(128)(4,1)} %bitcast.276), calls=%async_computation.17 | async-start | bytes 8388608 | tf_op jit(solution)/shard_map/while
  448.1 19.4 %slice-start.1 = ((s8[16777216]{0:T(1024)(128)(4,1)}), s8[4194304]{0:T(1024)(128)(4,1)S(1)}, s32[]{:S(2)}) async-start(s8[16777216]{0:T(1024)(128)(4,1)} %bitcast.276), calls=%async_computation.18 | async-start | bytes 8388608 | tf_op jit(solution)/shard_map/while
  453.4 14.1 slice-start.2
  460.0 7.5 slice-start.3
  469.1 6.2 copy-start.20
  469.1 6.2 copy-start.22
  484.5 28.5 %all-to-all-start.5 = ((bf16[2,1024,512]{2,0,1:T(2,128)(2,1)}), bf16[2,1024,512]{2,0,1:T(2,128)(2,1)}, u32[]{:S(2)}, u32[]{:S(2)}) async-start(bf16[2,1024,512]{2,0,1:T(2,128)(2,1)} %copy.59), calls=%async_computation.5 | async-start | bytes 4194304 | tf_op jit(solution)/shard_map/all_to_all | solution.py:228
  505.4 12.5 copy-start.35
  513.1 55.4 %all-to-all-start.6 = ((bf16[2,1024,512]{2,0,1:T(2,128)(2,1)}), bf16[2,1024,512]{2,0,1:T(2,128)(2,1)}, u32[]{:S(2)}, u32[]{:S(2)}) async-start(bf16[2,1024,512]{2,0,1:T(2,128)(2,1)} %copy.63), calls=%async_computation.6 | async-start | bytes 4194304 | tf_op jit(solution)/shard_map/all_to_all | solution.py:231
  568.4 53.7 %all-to-all-start.7 = ((bf16[2,1024,512]{2,0,1:T(2,128)(2,1)}), bf16[2,1024,512]{2,0,1:T(2,128)(2,1)}, u32[]{:S(2)}, u32[]{:S(2)}) async-start(bf16[2,1024,512]{2,0,1:T(2,128)(2,1)} %copy.67), calls=%async_computation.7 | async-start | bytes 4194304 | tf_op jit(solution)/shard_map/all_to_all | solution.py:234
  622.1 55.0 %all-to-all-start.3 = ((bf16[2,1024,512]{2,0,1:T(2,128)(2,1)}), bf16[2,1024,512]{2,0,1:T(2,128)(2,1)}, u32[]{:S(2)}, u32[]{:S(2)}) async-start(bf16[2,1024,512]{2,0,1:T(2,128)(2,1)} %copy.55), calls=%async_computation.3 | async-start | bytes 4194304 | tf_op jit(solution)/shard_map/all_to_all | solution.py:144
  627.0 177.0 %all-reduce.3.cloned.1.call-start = ((), (), s32[]{:S(2)}) async-start(), calls=%async_computation.16 | async-start | bytes 524288 | tf_op jit(solution)/shard_map/psum | solution.py:269
  627.0 5.9 copy-start.10
  627.0 5.9 copy-start.13
  627.1 5.9 copy-start.24
  627.1 5.9 copy-start.25
  627.1 5.9 copy-start.39
  642.2 13.2 copy-start.26
  642.3 13.2 copy-start.27
  642.3 13.2 copy-start.6
  642.3 13.2 copy-start.30
  642.3 13.2 copy-start.32
  642.3 13.2 copy-start.34
  655.5 15.7 copy-start.17
  676.9 269.9 %reduce-scatter.7.cloned.1.call-start = ((), (), s32[]{:S(2)}) async-start(), calls=%async_computation.13 | async-start | bytes 4325376 | tf_op jit(solution)/shard_map/reduce_scatter | solution.py:275
  677.2 5.8 copy-start.18
  687.4 418.5 %reduce-scatter.5.cloned.1.call-start = ((), (), s32[]{:S(2)}) async-start(), calls=%async_computation.12 | async-start | bytes 12976128 | tf_op jit(solution)/shard_map/reduce_scatter | solution.py:274
  700.3 764.9 %reduce-scatter.9.cloned.1.call-start = ((), (), s32[]{:S(2)}) async-start(), calls=%async_computation.14 | async-start | bytes 17301504 | tf_op jit(solution)/shard_map/reduce_scatter | solution.py:276
  717.0 1109.5 %reduce-scatter.11.cloned.1.call-start = ((), (), s32[]{:S(2)}) async-start(), calls=%async_computation.15 | async-start | bytes 17301504 | tf_op jit(solution)/shard_map/reduce_scatter | solution.py:277
  782.1 4.1 copy-start.7
  (13 other events, 22.3 us)
Sparse Core Ops, SparseCore 0:
  677.0 126.3 all-reduce.2
  806.2 140.5 reduce-scatter.6
  953.4 152.4 reduce-scatter.4
  1108.8 356.4 reduce-scatter.8
  1468.1 358.4 reduce-scatter.10
where the time goes:
time: 1840 us; the launch traced here: 1830 us
  waiting for transfers between devices  1060 us (58%)
  matrix products  344 us (19%)
  local copies, waits for them, and re-layouts  210 us (11%)
  other arithmetic  124 us (7%)
  blocking collectives  41.9 us (2%)
  starting transfers between devices  39.8 us (2%)
    reduce_scatter x1, waiting for transfers between devices, body(): lax.psum_scatter(down_grad, ('dp', 'seq'), scatter_dimension=0, tiled=True)  361 us
    reduce_scatter x1, waiting for transfers between devices, body(): lax.psum_scatter(up_grad, ('dp', 'seq'), scatter_dimension=0, tiled=True)  359 us
    reduce_scatter x1, waiting for transfers between devices, body(): lax.psum_scatter(qkv_grad, ('dp', 'seq'), scatter_dimension=0, tiled=True)  159 us
    reduce_scatter x1, waiting for transfers between devices, body(): lax.psum_scatter(out_grad, ('dp', 'seq'), scatter_dimension=0, tiled=True)  143 us
    dot_general x8, matrix products, scores_for(): jnp.einsum('qhd,khd->hqk', query_block, key_rows, preferred_element_type=...  71.4 us
    convert_element_type x4, other arithmetic, attend_back(): scores_grad = (probs_full * (probs_grad - inner_sum)).astype(jnp.bfloat16)  45.3 us
    psum x1, blocking collectives, body(): lax.psum((gain_grad, bias_grad, up_bias_grad, down_bias_grad, family_grad...  41.9 us
  transfers between devices with their start and end apart: 13, of which 7 were waited for; matrix products, arithmetic and copies ran while one was open for 21% of the time, Pallas kernels for 0%

commit v1 on v0

--- a/solution.py
+++ b/solution.py
@@ -1,13 +1,20 @@
+import functools
 import math
 
 import jax
 import jax.numpy as jnp
 from jax import lax
+from jax.experimental import pallas as pl
+from jax.experimental.pallas import tpu as pltpu
 from jax.sharding import PartitionSpec as P
 
 H = 16
 HD = 64
 ROT = 32
+MESH = pl.DeviceIdType.MESH
+VMEM_LIMIT = 60 * 1024 * 1024
+F32 = jnp.float32
+BF16 = jnp.bfloat16
 
 
 def for_sending(shard):
@@ -47,7 +54,7 @@
     return jax.nn.gelu(pre_values, approximate=True)
 
 
-def body(
+def body_by_heads(
     hidden_in,
     family,
     orient,
@@ -292,6 +299,775 @@
     )
 
 
+def dot_nn(a, b):
+    return lax.dot_general(a, b, (((1,), (0,)), ((), ())), preferred_element_type=F32)
+
+
+def dot_nt(a, b):
+    return lax.dot_general(a, b, (((1,), (1,)), ((), ())), preferred_element_type=F32)
+
+
+def dot_tn(a, b):
+    return lax.dot_general(a, b, (((0,), (0,)), ((), ())), preferred_element_type=F32)
+
+
+def params(**more):
+    return pltpu.CompilerParams(vmem_limit_bytes=VMEM_LIMIT, **more)
+
+
+def cost(flops, moved, exps=0):
+    return pl.CostEstimate(flops=flops, bytes_accessed=moved, transcendentals=exps)
+
+
+def whole(shape):
+    return pl.BlockSpec(shape, lambda *_: (0,) * len(shape), pipeline_mode=pl.Buffered(1))
+
+
+def table_row(table, wanted):
+    rows = lax.broadcasted_iota(jnp.int32, table.shape, 0)
+    return jnp.sum(jnp.where(rows == wanted, table[...].astype(F32), 0.0), 0, keepdims=True)
+
+
+def normalise(entries):
+    centred = entries - jnp.mean(entries, -1, keepdims=True)
+    inv_std = lax.rsqrt(jnp.mean(centred * centred, -1, keepdims=True) + 1e-05)
+    return centred * inv_std, inv_std
+
+
+GELU_C = math.sqrt(2.0 / math.pi)
+
+
+def gelu_both(z):
+    square = z * z
+    t = jnp.tanh(GELU_C * z * (1.0 + 0.044715 * square))
+    half = 0.5 * (1.0 + t)
+    slope = half + (0.5 * GELU_C) * z * (1.0 - t * t) * (1.0 + (3 * 0.044715) * square)
+    return z * half, slope
+
+
+def ffn_kernel(rows, ids, hid, cot, fam, ori, gain, bias, wup, bup, wdn, norm, act, pre, bupg, bdng):
+    tokens = hid.shape[0]
+    seg = tokens // rows
+    step = 256
+
+    @pl.when(pl.program_id(0) == 0)
+    def _():
+        total = jnp.zeros((1, cot.shape[1]), F32)
+        for row in range(rows):
+            emb = table_row(fam, ids[0]) + table_row(ori, ids[1 + row])
+            for start in range(row * seg, (row + 1) * seg, step):
+                part = pl.ds(start, step)
+                hat, _ = normalise(hid[part, :].astype(F32) + emb)
+                norm[part, :] = (hat * gain[...].astype(F32) + bias[...].astype(F32)).astype(BF16)
+                total = total + jnp.sum(cot[part, :].astype(F32), 0, keepdims=True)
+        bdng[...] = total
+
+    total = jnp.zeros((1, wup.shape[1]), F32)
+    for start in range(0, tokens, step):
+        part = pl.ds(start, step)
+        z = dot_nn(norm[part, :], wup[...]) + bup[...].astype(F32)
+        into = dot_nt(cot[part, :], wdn[...])
+        value, slope = gelu_both(z)
+        act[part, :] = value.astype(BF16)
+        low = (into * slope).astype(BF16)
+        pre[part, :] = low
+        total = total + jnp.sum(low.astype(F32), 0, keepdims=True)
+    bupg[...] = total
+
+
+def ffn_forward(ids, hid, cot, fam, ori, gain, bias, wup, bup, wdn, rows):
+    tokens, d = hid.shape
+    ff = wup.shape[1]
+    tile = 512
+    return pl.pallas_call(
+        functools.partial(ffn_kernel, rows),
+        grid_spec=pltpu.PrefetchScalarGridSpec(
+            num_scalar_prefetch=1,
+            grid=(ff // tile,),
+            in_specs=[
+                whole((tokens, d)),
+                whole((tokens, d)),
+                whole(fam.shape),
+                whole(ori.shape),
+                whole((1, d)),
+                whole((1, d)),
+                pl.BlockSpec((d, tile), lambda i, s: (0, i)),
+                pl.BlockSpec((1, tile), lambda i, s: (0, i)),
+                pl.BlockSpec((tile, d), lambda i, s: (i, 0)),
+            ],
+            out_specs=[
+                whole((tokens, d)),
+                pl.BlockSpec((tokens, tile), lambda i, s: (0, i)),
+                pl.BlockSpec((tokens, tile), lambda i, s: (0, i)),
+                pl.BlockSpec((1, tile), lambda i, s: (0, i)),
+                whole((1, d)),
+            ],
+        ),
+        out_shape=[
+            jax.ShapeDtypeStruct((tokens, d), BF16),
+            jax.ShapeDtypeStruct((tokens, ff), BF16),
+            jax.ShapeDtypeStruct((tokens, ff), BF16),
+            jax.ShapeDtypeStruct((1, ff), F32),
+            jax.ShapeDtypeStruct((1, d), F32),
+        ],
+        compiler_params=params(),
+        cost_estimate=cost(4 * tokens * d * ff, 4 * tokens * ff + 4 * d * ff, tokens * ff),
+        name="ffn_forward",
+    )(ids, hid, cot, fam, ori, gain, bias, wup, bup, wdn)
+
+
+def turn(entries, cosine, sine):
+    even = lax.broadcasted_iota(jnp.int32, entries.shape, 1) % 2 == 0
+    other = jnp.where(even, pltpu.roll(entries, 127, 1), pltpu.roll(entries, 1, 1))
+    return entries * cosine + other * sine
+
+
+def turn_back(entries, cosine, sine):
+    even = lax.broadcasted_iota(jnp.int32, entries.shape, 1) % 2 == 0
+    side = entries * sine
+    other = jnp.where(even, pltpu.roll(side, 127, 1), pltpu.roll(side, 1, 1))
+    return entries * cosine + other
+
+
+def qkv_kernel(tiles, ids, own, far, cown, cfar, fam, ori, gain, bias, wqkv, wout, cos, sin, norm, cot, qkv, datt):
+    seg = own.shape[0]
+    step = 256
+    i = pl.program_id(0)
+    me = ids[1]
+
+    @pl.when(i == 0)
+    def _():
+        emb = table_row(fam, ids[0]) + table_row(ori, ids[2])
+        for source, csource, where in ((own, cown, me), (far, cfar, 1 - me)):
+            for start in range(0, seg, step):
+                part = pl.ds(start, step)
+                there = pl.ds(pl.multiple_of(where * seg + start, step), step)
+                hat, _ = normalise(source[part, :].astype(F32) + emb)
+                norm[there, :] = (hat * gain[...].astype(F32) + bias[...].astype(F32)).astype(BF16)
+                cot[there, :] = csource[part, :]
+
+    @pl.when(i < 2 * tiles)
+    def _():
+        for start in range(0, 2 * seg, step):
+            part = pl.ds(start, step)
+            lin = dot_nn(norm[part, :], wqkv[...])
+            for lane in range(0, lin.shape[1], 128):
+                piece = turn(lin[:, lane : lane + 128], cos[part, :], sin[part, :])
+                qkv[part, lane : lane + 128] = piece.astype(BF16)
+
+    @pl.when((i >= 2 * tiles) & (i < 3 * tiles))
+    def _():
+        for start in range(0, 2 * seg, step):
+            part = pl.ds(start, step)
+            qkv[part, :] = dot_nn(norm[part, :], wqkv[...]).astype(BF16)
+
+    @pl.when(i >= 3 * tiles)
+    def _():
+        for start in range(0, 2 * seg, step):
+            part = pl.ds(start, step)
+            datt[part, :] = dot_nt(cot[part, :], wout[...]).astype(BF16)
+
+
+def qkv_forward(ids, own, far, cown, cfar, fam, ori, gain, bias, wqkv, wout, cos, sin):
+    seg, d = own.shape
+    full = 2 * seg
+    tile = 512
+    tiles = d // tile
+    return pl.pallas_call(
+        functools.partial(qkv_kernel, tiles),
+        grid_spec=pltpu.PrefetchScalarGridSpec(
+            num_scalar_prefetch=1,
+            grid=(4 * tiles,),
+            in_specs=[
+                whole((seg, d)),
+                whole((seg, d)),
+                whole((seg, d)),
+                whole((seg, d)),
+                whole(fam.shape),
+                whole(ori.shape),
+                whole((1, d)),
+                whole((1, d)),
+                pl.BlockSpec((d, tile), lambda i, s: (0, jnp.minimum(i, 3 * tiles - 1))),
+                pl.BlockSpec((tile, d), lambda i, s: (jnp.maximum(i - 3 * tiles, 0), 0)),
+                whole((full, 128)),
+                whole((full, 128)),
+            ],
+            out_specs=[
+                whole((full, d)),
+                whole((full, d)),
+                pl.BlockSpec((full, tile), lambda i, s: (0, jnp.minimum(i, 3 * tiles - 1))),
+                pl.BlockSpec((full, tile), lambda i, s: (0, jnp.maximum(i - 3 * tiles, 0))),
+            ],
+        ),
+        out_shape=[
+            jax.ShapeDtypeStruct((full, d), BF16),
+            jax.ShapeDtypeStruct((full, d), BF16),
+            jax.ShapeDtypeStruct((full, 3 * d), BF16),
+            jax.ShapeDtypeStruct((full, d), BF16),
+        ],
+        compiler_params=params(),
+        cost_estimate=cost(8 * full * d * d, 8 * d * d + 18 * full * d),
+        name="qkv_forward",
+    )(ids, own, far, cown, cfar, fam, ori, gain, bias, wqkv, wout, cos, sin)
+
+
+def attention_kernel(head_size, q_ref, k_ref, v_ref, g_ref, cos, sin, o_ref, dq_ref, dk_ref, dv_ref, dkt, dvt):
+    full = q_ref.shape[0]
+    block = 256
+    scale = head_size ** (-0.5)
+    lane = lax.broadcasted_iota(jnp.int32, (block, 128), 1)
+    below = lax.broadcasted_iota(jnp.int32, (block, block), 0) >= lax.broadcasted_iota(
+        jnp.int32, (block, block), 1
+    )
+    dkt[...] = jnp.zeros_like(dkt)
+    dvt[...] = jnp.zeros_like(dvt)
+    for start in range(0, full, block):
+        part = pl.ds(start, block)
+        end = start + block
+        query = q_ref[part, :]
+        grad = g_ref[part, :]
+        out = None
+        dq = None
+        for head in range(128 // head_size):
+            mine = (lane >= head * head_size) & (lane < (head + 1) * head_size)
+            qm = jnp.where(mine, query.astype(F32) * scale, 0.0).astype(BF16)
+            gm = jnp.where(mine, grad.astype(F32), 0.0).astype(BF16)
+            scores = dot_nt(qm, k_ref[0:end, :])
+            last = jnp.where(below, scores[:, start:end], -1e30)
+            scores = last if start == 0 else jnp.concatenate([scores[:, :start], last], 1)
+            weights = jnp.exp(scores - jnp.max(scores, -1, keepdims=True))
+            probs = weights * (1.0 / jnp.sum(weights, -1, keepdims=True))
+            low = probs.astype(BF16)
+            piece = dot_nn(low, v_ref[0:end, :])
+            out = piece if out is None else jnp.where(mine, piece, out)
+            pg = dot_nt(gm, v_ref[0:end, :])
+            inner = jnp.sum(probs * pg, -1, keepdims=True)
+            sg = (probs * (pg - inner)).astype(BF16)
+            piece = dot_nn(sg, k_ref[0:end, :])
+            dq = piece if dq is None else jnp.where(mine, piece, dq)
+            dkt[:, 0:end] += dot_tn(qm, sg)
+            dvt[:, 0:end] += dot_tn(gm, low)
+        o_ref[part, :] = out.astype(BF16)
+        dq_ref[part, :] = turn_back(dq * scale, cos[part, :], sin[part, :]).astype(BF16)
+    for start in range(0, full, block):
+        part = pl.ds(start, block)
+        dk = dkt[:, start : start + block].T
+        dk_ref[part, :] = turn_back(dk, cos[part, :], sin[part, :]).astype(BF16)
+        dv_ref[part, :] = dvt[:, start : start + block].T.astype(BF16)
+
+
+def attention(qkv, datt, cos, sin, head_size):
+    full, d = datt.shape
+    pairs = d // 128
+    shape = jax.ShapeDtypeStruct((full, d), BF16)
+    spec = pl.BlockSpec((full, 128), lambda i: (0, i))
+    return pl.pallas_call(
+        functools.partial(attention_kernel, head_size),
+        grid=(pairs,),
+        in_specs=[
+            spec,
+            pl.BlockSpec((full, 128), lambda i: (0, pairs + i)),
+            pl.BlockSpec((full, 128), lambda i: (0, 2 * pairs + i)),
+            spec,
+            whole((full, 128)),
+            whole((full, 128)),
+        ],
+        out_specs=[spec] * 4,
+        out_shape=[shape] * 4,
+        scratch_shapes=[pltpu.VMEM((128, full), F32), pltpu.VMEM((128, full), F32)],
+        compiler_params=params(),
+        cost_estimate=cost(12 * full * full * d * 2, 16 * full * d, full * full * H),
+        name="attention",
+    )(qkv, qkv, qkv, datt, cos, sin)
+
+
+def store_blocks(meta, value, keep, send, upper, seqs):
+    size = keep.shape[-2]
+    core = meta[0]
+    for up in range(upper):
+        for seq in range(seqs):
+            first = (up * 2 * seqs + seq) * size
+            second = first + seqs * size
+            a = value[first : first + size, :].astype(BF16)
+            b = value[second : second + size, :].astype(BF16)
+            at = meta[2 + up] if upper > 1 else 0
+            there = lax.rem(meta[1] + seq, 2)
+            keep[at, there] = jnp.where(core == 0, a, b)
+            send[at, there] = jnp.where(core == 0, b, a)
+
+
+def up_grad_kernel(meta, left, right, keep, send, turned):
+    @pl.when(pl.program_id(0) == 0)
+    def _():
+        turned[...] = left[...].T
+
+    store_blocks(meta, dot_nn(turned[...], right[...]), keep, send, keep.shape[0], 2)
+
+
+def up_grad(meta, left, right, upper):
+    tokens, d = left.shape
+    n = right.shape[1]
+    tile = 512
+    size = d // (upper * 4)
+    shape = jax.ShapeDtypeStruct((upper, 2, size, n), BF16)
+    spec = pl.BlockSpec((upper, 2, size, tile), lambda j, s: (0, 0, 0, j))
+    return pl.pallas_call(
+        up_grad_kernel,
+        grid_spec=pltpu.PrefetchScalarGridSpec(
+            num_scalar_prefetch=1,
+            grid=(n // tile,),
+            in_specs=[whole((tokens, d)), pl.BlockSpec((tokens, tile), lambda j, s: (0, j))],
+            out_specs=[spec, spec],
+            scratch_shapes=[pltpu.VMEM((d, tokens), BF16)],
+        ),
+        out_shape=[shape, shape],
+        compiler_params=params(),
+        cost_estimate=cost(2 * tokens * d * n, 2 * (tokens * n + d * n + tokens * d)),
+        name="up_grad",
+    )(meta, left, right)
+
+
+def down_grad_kernel(meta, left, right, keep, send):
+    store_blocks(meta, dot_nn(left[...].T, right[...]), keep, send, 1, 2)
+
+
+def down_grad(meta, left, right, upper):
+    tokens, m = left.shape
+    d = right.shape[1]
+    tile = m // upper
+    size = tile // 4
+    shape = jax.ShapeDtypeStruct((upper, 2, size, d), BF16)
+    spec = pl.BlockSpec((1, 2, size, d), lambda i, s: (s[2 + i], 0, 0, 0))
+    return pl.pallas_call(
+        down_grad_kernel,
+        grid_spec=pltpu.PrefetchScalarGridSpec(
+            num_scalar_prefetch=1,
+            grid=(upper,),
+            in_specs=[pl.BlockSpec((tokens, tile), lambda i, s: (0, i)), whole((tokens, d))],
+            out_specs=[spec, spec],
+        ),
+        out_shape=[shape, shape],
+        compiler_params=params(),
+        cost_estimate=cost(2 * tokens * d * m, 2 * (tokens * m + d * m + tokens * d)),
+        name="down_grad",
+    )(meta, left, right)
+
+
+def late_grad_kernel(tiles, meta, att, cot, norm, dq, dk, dv, keep, send, turned):
+    j = pl.program_id(0)
+
+    @pl.when(j == 0)
+    def _():
+        turned[...] = att[...].T
+
+    @pl.when(j == tiles)
+    def _():
+        turned[...] = norm[...].T
+
+    for index, right in enumerate((cot, dq, dk, dv)):
+
+        @pl.when((j >= index * tiles) & (j < (index + 1) * tiles))
+        def _():
+            store_blocks(meta, dot_nn(turned[...], right[...]), keep, send, keep.shape[0], 2)
+
+
+def late_grad(meta, att, cot, norm, dq, dk, dv, upper):
+    tokens, d = att.shape
+    tile = 512
+    tiles = d // tile
+    size = d // (upper * 4)
+    shape = jax.ShapeDtypeStruct((upper, 2, size, 4 * d), BF16)
+    spec = pl.BlockSpec((upper, 2, size, tile), lambda j, s: (0, 0, 0, j))
+
+    def part(index):
+        return pl.BlockSpec(
+            (tokens, tile), lambda j, s: (0, jnp.clip(j - index * tiles, 0, tiles - 1))
+        )
+
+    return pl.pallas_call(
+        functools.partial(late_grad_kernel, tiles),
+        grid_spec=pltpu.PrefetchScalarGridSpec(
+            num_scalar_prefetch=1,
+            grid=(4 * tiles,),
+            in_specs=[whole((tokens, d)), part(0), whole((tokens, d)), part(1), part(2), part(3)],
+            out_specs=[spec, spec],
+            scratch_shapes=[pltpu.VMEM((d, tokens), BF16)],
+        ),
+        out_shape=[shape, shape],
+        compiler_params=params(),
+        cost_estimate=cost(8 * tokens * d * d, 20 * tokens * d),
+        name="late_grad",
+    )(meta, att, cot, norm, dq, dk, dv)
+
+
+def reduce_blocks(keep, send):
+    bits = int(math.log2(lax.axis_size("dp")))
+
+    def swap(bit):
+        return [(i, i ^ (1 << bit)) for i in range(1 << bits)]
+
+    keep = keep.reshape((-1,) + keep.shape[2:])
+    got = lax.ppermute(send, "dp", swap(0)).reshape(keep.shape)
+    for bit in range(1, bits):
+        half = keep.shape[0] // 2
+        send = (keep[half:].astype(F32) + got[half:].astype(F32)).astype(BF16)
+        keep = (keep[:half].astype(F32) + got[:half].astype(F32)).astype(BF16)
+        got = lax.ppermute(send, "dp", swap(bit))
+    send = (keep[1].astype(F32) + got[1].astype(F32)).astype(BF16)
+    keep = keep[0].astype(F32) + got[0].astype(F32)
+    return keep + lax.ppermute(send, "seq", [(0, 1), (1, 0)]).astype(F32)
+
+
+def back_kernel(dq, dk, dv, w, out):
+    d = dq.shape[1]
+    total = dot_nt(dq[...], w[:, 0:d])
+    total = total + dot_nt(dk[...], w[:, d : 2 * d])
+    total = total + dot_nt(dv[...], w[:, 2 * d : 3 * d])
+    out[...] = total.astype(BF16)
+
+
+def project_back(dq, dk, dv, w):
+    tokens, d = dq.shape
+    step = 256
+    spec = pl.BlockSpec((step, d), lambda i: (i, 0))
+    return pl.pallas_call(
+        back_kernel,
+        grid=(tokens // step,),
+        in_specs=[spec, spec, spec, whole(w.shape)],
+        out_specs=spec,
+        out_shape=jax.ShapeDtypeStruct((tokens, d), BF16),
+        compiler_params=params(),
+        cost_estimate=cost(6 * tokens * d * d, 6 * d * d + 8 * tokens * d),
+        name="project_back",
+    )(dq, dk, dv, w)
+
+
+def out_kernel(per_row, ids, hid, fam, ori, act, wdn, own, far, wout, bdn, out):
+    row = pl.program_id(0) // per_row
+    emb = table_row(fam, ids[0]) + table_row(ori, ids[2 + row])
+    att = jnp.where(row == ids[1], own[...], far[...])
+    total = hid[...].astype(F32) + emb + dot_nn(att, wout[...])
+    total = total + (dot_nn(act[...], wdn[...]) + bdn[...].astype(F32))
+    out[...] = total.astype(BF16)
+
+
+def input_kernel(per_row, ids, hid, fam, ori, pre, wup, own, far, gain, cot, out, gg, bg, rg):
+    i = pl.program_id(0)
+    row = i // per_row
+    emb = table_row(fam, ids[0]) + table_row(ori, ids[2 + row])
+    hat, inv_std = normalise(hid[...].astype(F32) + emb)
+    grad = dot_nt(pre[...], wup[...]) + jnp.where(row == ids[1], own[...], far[...]).astype(F32)
+
+    @pl.when(i == 0)
+    def _():
+        gg[...] = jnp.zeros_like(gg)
+        bg[...] = jnp.zeros_like(bg)
+        rg[...] = jnp.zeros_like(rg)
+
+    gg[...] += jnp.sum(grad * hat, 0, keepdims=True)
+    bg[...] += jnp.sum(grad, 0, keepdims=True)
+    scaled = grad * gain[...].astype(F32)
+    inner = (
+        scaled
+        - jnp.mean(scaled, -1, keepdims=True)
+        - hat * jnp.mean(scaled * hat, -1, keepdims=True)
+    )
+    result = cot[...].astype(F32) + inv_std * inner
+    out[...] = result
+    sums = jnp.sum(result, 0, keepdims=True)
+    rows = lax.broadcasted_iota(jnp.int32, rg.shape, 0)
+    rg[...] += jnp.where(rows == row, sums, 0.0)
+
+
+def home_specs(tokens, d, rows, step):
+    per_row = tokens // rows // step
+    local = pl.BlockSpec((step, d), lambda i, s: (i, 0))
+    own = pl.BlockSpec((step, d), lambda i, s: (s[1] * per_row + i % per_row, 0))
+    far = pl.BlockSpec((step, d), lambda i, s: (i % per_row, 0))
+    return per_row, local, own, far
+
+
+def layer_output(ids, hid, fam, ori, act, wdn, own, far, wout, bdn, rows):
+    tokens, d = hid.shape
+    ff = act.shape[1]
+    step = 256
+    per_row, local, own_spec, far_spec = home_specs(tokens, d, rows, step)
+    return pl.pallas_call(
+        functools.partial(out_kernel, per_row),
+        grid_spec=pltpu.PrefetchScalarGridSpec(
+            num_scalar_prefetch=1,
+            grid=(tokens // step,),
+            in_specs=[
+                local,
+                whole(fam.shape),
+                whole(ori.shape),
+                pl.BlockSpec((step, ff), lambda i, s: (i, 0)),
+                whole(wdn.shape),
+                own_spec,
+                far_spec,
+                whole(wout.shape),
+                whole((1, d)),
+            ],
+            out_specs=local,
+        ),
+        out_shape=jax.ShapeDtypeStruct((tokens, d), BF16),
+        compiler_params=params(),
+        cost_estimate=cost(2 * tokens * d * (ff + d), 2 * (d * (ff + d) + tokens * ff + 4 * tokens * d)),
+        name="layer_output",
+    )(ids, hid, fam, ori, act, wdn, own, far, wout, bdn)
+
+
+def input_gradient(ids, hid, fam, ori, pre, wup, own, far, gain, cot, rows):
+    tokens, d = hid.shape
+    ff = pre.shape[1]
+    step = 256
+    per_row, local, own_spec, far_spec = home_specs(tokens, d, rows, step)
+    return pl.pallas_call(
+        functools.partial(input_kernel, per_row),
+        grid_spec=pltpu.PrefetchScalarGridSpec(
+            num_scalar_prefetch=1,
+            grid=(tokens // step,),
+            in_specs=[
+                local,
+                whole(fam.shape),
+                whole(ori.shape),
+                pl.BlockSpec((step, ff), lambda i, s: (i, 0)),
+                whole(wup.shape),
+                own_spec,
+                far_spec,
+                whole((1, d)),
+                local,
+            ],
+            out_specs=[local, whole((1, d)), whole((1, d)), whole((rows, d))],
+        ),
+        out_shape=[
+            jax.ShapeDtypeStruct((tokens, d), F32),
+            jax.ShapeDtypeStruct((1, d), F32),
+            jax.ShapeDtypeStruct((1, d), F32),
+            jax.ShapeDtypeStruct((rows, d), F32),
+        ],
+        compiler_params=params(),
+        cost_estimate=cost(2 * tokens * d * ff, 2 * (d * ff + tokens * ff + 6 * tokens * d)),
+        name="input_gradient",
+    )(ids, hid, fam, ori, pre, wup, own, far, gain, cot)
+
+
+def sums_kernel(bits, sums_ref, vec_ref, sums_out, all_out, held, got, vgot, send_sem, recv_sem, gsend, grecv):
+    dp = lax.axis_index("dp")
+    seq = lax.axis_index("seq")
+    partners = [(dp, 1 - seq)]
+    for bit in range(bits):
+        size = 1 << bit
+        partners.append((dp + (1 - 2 * lax.rem(dp // size, 2)) * size, seq))
+    barrier = pltpu.get_barrier_semaphore()
+    for partner in partners:
+        pl.semaphore_signal(barrier, inc=1, device_id=partner, device_id_type=MESH)
+    pl.semaphore_wait(barrier, len(partners))
+
+    def remote(src, dst, send, recv, partner):
+        copy = pltpu.make_async_remote_copy(
+            src_ref=src, dst_ref=dst, send_sem=send, recv_sem=recv, device_id=partner, device_id_type=MESH
+        )
+        copy.start()
+        return copy
+
+    for index, partner in enumerate(partners):
+        source = sums_ref if index == 0 else held.at[index]
+        main = remote(source, got.at[index], send_sem.at[index], recv_sem.at[index], partner)
+        if index == 0:
+            side = remote(vec_ref, vgot, gsend.at[0], grecv.at[0], partner)
+        else:
+            size = 1 << (index - 1)
+            held_now = pl.ds(dp - lax.rem(dp, size), size)
+            side = remote(
+                all_out.at[held_now], all_out.at[held_now], gsend.at[index], grecv.at[index], partner
+            )
+        main.wait()
+        total = source[...] + got[index]
+        if index + 1 < len(partners):
+            held[index + 1] = total
+        else:
+            sums_out[...] = total
+        side.wait()
+        if index == 0:
+            all_out[dp] = vec_ref[...] + vgot[...]
+
+
+def sum_small(sums, vec):
+    count = lax.axis_size("dp")
+    bits = int(math.log2(count))
+    rounds = bits + 1
+    return pl.pallas_call(
+        functools.partial(sums_kernel, bits),
+        in_specs=[pl.BlockSpec(memory_space=pltpu.VMEM)] * 2,
+        out_specs=[pl.BlockSpec(memory_space=pltpu.VMEM)] * 2,
+        out_shape=[
+            jax.ShapeDtypeStruct(sums.shape, F32),
+            jax.ShapeDtypeStruct((count,) + vec.shape, F32),
+        ],
+        scratch_shapes=[
+            pltpu.VMEM((rounds,) + sums.shape, F32),
+            pltpu.VMEM((rounds,) + sums.shape, F32),
+            pltpu.VMEM(vec.shape, F32),
+            pltpu.SemaphoreType.DMA((rounds,)),
+            pltpu.SemaphoreType.DMA((rounds,)),
+            pltpu.SemaphoreType.DMA((rounds,)),
+            pltpu.SemaphoreType.DMA((rounds,)),
+        ],
+        compiler_params=pltpu.CompilerParams(collective_id=0, has_side_effects=True),
+        name="sum_small",
+    )(sums, vec)
+
+
+def body_by_rows(
+    hidden_in,
+    family,
+    orient,
+    norm_gain,
+    norm_bias,
+    qkv_weight,
+    out_weight,
+    up_weight,
+    up_bias,
+    down_weight,
+    down_bias,
+    family_table,
+    orient_table,
+    cotangent,
+):
+    rows, seg, d = hidden_in.shape
+    ff = up_weight.shape[1]
+    tokens = rows * seg
+    full = 2 * seg
+    dp_count = lax.axis_size("dp")
+    bits = int(math.log2(dp_count))
+    upper = dp_count // 2
+    dp = lax.axis_index("dp")
+    seq = lax.axis_index("seq")
+    ring = [(0, 1), (1, 0)]
+
+    def mine(pair):
+        return lax.dynamic_index_in_dim(pair, seq, 0, keepdims=False)
+
+    def theirs(pair):
+        return lax.dynamic_index_in_dim(pair, 1 - seq, 0, keepdims=False)
+
+    far_hidden = lax.ppermute(theirs(hidden_in), "seq", ring)
+    far_cot = lax.ppermute(theirs(cotangent), "seq", ring)
+
+    gain = norm_gain.reshape(1, d)
+    bias = norm_bias.reshape(1, d)
+    hid = hidden_in.reshape(tokens, d)
+    cot = cotangent.reshape(tokens, d)
+    ids = jnp.concatenate([family, orient])
+    tail_ids = jnp.concatenate([family, seq[None].astype(jnp.int32), orient])
+    row_ids = jnp.stack([family[0], seq.astype(jnp.int32), mine(orient)])
+
+    group = jnp.arange(upper, dtype=jnp.int32) ^ (dp // 2)
+    place = jnp.zeros_like(group)
+    for bit in range(bits - 1):
+        place = place + (((group >> bit) & 1) << (bits - 2 - bit))
+    meta = jnp.concatenate([jnp.stack([dp % 2, seq]).astype(jnp.int32), place])
+
+    normed, act, pre, up_bias_part, down_bias_part = ffn_forward(
+        ids, hid, cot, family_table, orient_table, gain, bias, up_weight, up_bias.reshape(1, ff), down_weight, rows
+    )
+    up_keep, up_send = up_grad(meta, normed, pre, upper)
+    down_keep, down_send = down_grad(meta, act, cot, upper)
+    up_total = reduce_blocks(up_keep, up_send)
+    down_total = reduce_blocks(down_keep, down_send)
+
+    cosine, sine = rope_tables(jnp.arange(full).astype(F32), 128)
+    row_normed, row_cot, qkv, datt = qkv_forward(
+        row_ids,
+        mine(hidden_in),
+        far_hidden,
+        mine(cotangent),
+        far_cot,
+        family_table,
+        orient_table,
+        gain,
+        bias,
+        qkv_weight,
+        out_weight,
+        cosine,
+        sine,
+    )
+    att, dq, dk, dv = attention(qkv, datt, cosine, sine, d // H)
+    keep, send = late_grad(meta, att, row_cot, row_normed, dq, dk, dv, upper)
+    late_total = reduce_blocks(keep, send)
+    far_att = lax.ppermute(theirs(att.reshape(2, seg, d)), "seq", ring)
+    back = project_back(dq, dk, dv, qkv_weight)
+    far_back = lax.ppermute(theirs(back.reshape(2, seg, d)), "seq", ring)
+
+    layer_out = layer_output(
+        tail_ids,
+        hid,
+        family_table,
+        orient_table,
+        act,
+        down_weight,
+        att,
+        far_att,
+        out_weight,
+        down_bias.reshape(1, d),
+        rows,
+    )
+    input_grad, gain_part, bias_part, row_part = input_gradient(
+        tail_ids, hid, family_table, orient_table, pre, up_weight, back, far_back, gain, cot, rows
+    )
+
+    flag = orient[0]
+    by_flag = jnp.where(flag == 0, row_part, row_part[::-1])
+    packed = jnp.concatenate(
+        [
+            part.reshape(-1, 128)
+            for part in (up_bias_part, down_bias_part, gain_part, bias_part, by_flag)
+        ],
+        0,
+    )
+    vec = jnp.concatenate(
+        [
+            (row_part[0] + row_part[1]).reshape(-1, 128),
+            jnp.full((8, 128), 0.5, F32) * family.astype(F32)[0],
+        ],
+        0,
+    )
+    sums, gathered = sum_small(packed, vec)
+    flat = sums.reshape(-1)
+    up_bias_sum = flat[:ff]
+    down_bias_sum, gain_sum, bias_sum = flat[ff : ff + 3 * d].reshape(3, d)
+    orient_sum = flat[ff + 3 * d :].reshape(2, d)
+    families = family_table.shape[0]
+    hot = gathered[:, -1, 0].astype(jnp.int32)[None, :] == jnp.arange(families)[:, None]
+    family_sum = jnp.dot(
+        hot.astype(F32), gathered[:, :-8].reshape(dp_count, d), precision=lax.Precision.HIGHEST
+    )
+    return (
+        layer_out.reshape(rows, seg, d),
+        input_grad.reshape(rows, seg, d),
+        gain_sum,
+        bias_sum,
+        late_total[:, d:],
+        late_total[:, :d],
+        up_total,
+        up_bias_sum,
+        down_total,
+        down_bias_sum,
+        family_sum,
+        orient_sum,
+    )
+
+
+def body(*args):
+    hidden_in = args[0]
+    dp_count = lax.axis_size("dp")
+    two_rows = lax.axis_size("seq") == 2 and hidden_in.shape[0] == 2
+    if two_rows and dp_count >= 4 and dp_count & (dp_count - 1) == 0:
+        return body_by_rows(*args)
+    return body_by_heads(*args)
+
+
 def solution(mesh):
     return jax.shard_map(
         body,

time: 1840 us -> 512 us (0.28)
  waiting for transfers between devices: 1060 us -> 192 us
  matrix products: 344 us -> 0.96 us
  Pallas kernels: 0 us -> 240 us
  local copies, waits for them, and re-layouts: 210 us -> 23.8 us
  other arithmetic: 124 us -> 25.6 us
  blocking collectives: 41.9 us -> 0 us
  starting transfers between devices: 39.8 us -> 18.2 us
    reduce_scatter x4 -> x0, waiting for transfers between devices: 1020 us -> none  [the longest x1 361 us: body(): lax.psum_scatter(down_grad, ('dp', 'seq'), scatter_dimension=0, tiled=True)]
    dot_general x44 -> x1, matrix products: 344 us -> 0.96 us  [body_by_rows(): jnp.dot(hot.astype(F32), gathered[:, :-8].reshape(dp_count, d), precision...]
    pallas_call x0 -> x10, Pallas kernels: none -> 240 us  [the longest x1 66.7 us: attention(): pl.pallas_call(functools.partial(attention_kernel, head_size), grid=(pair...]
    ppermute x0 -> x19, waiting for transfers between devices: none -> 192 us  [the longest x9 184 us: reduce_blocks(): got = lax.ppermute(send, 'dp', swap(bit))]
    convert_element_type x9 -> x0, local copies, waits for them, and re-layouts: 53 us -> none  [the longest x3 18.5 us: body(): query_grad_pos.astype(jnp.float32)]
    convert_element_type x11 -> x14, other arithmetic: 62.7 us -> 16.8 us  [the longest x9 15.4 us: reduce_blocks(): keep = (keep[:half].astype(F32) + got[:half].astype(F32)).astype(BF16)]
    all_to_all x9 -> x0, local copies, waits for them, and re-layouts: 42.1 us -> none  [the longest x2 9.65 us: body(): lax.all_to_all(values, 'seq', split_axis=2, concat_axis=1, tiled=True)]
    psum x1 -> x0, blocking collectives: 41.9 us -> none  [body(): lax.psum((gain_grad, bias_grad, up_bias_grad, down_bias_grad, family_grad...]
  transfers between devices with their start and end apart: 13 -> 19, of which waited for: 7 -> 8; matrix products, arithmetic and copies ran while one was open for 21% -> 8% of each run, Pallas kernels for 0% -> 48%
where the time goes in v1:
time: 512 us; the launch traced here: 504 us
  Pallas kernels  240 us (47%)
  waiting for transfers between devices  192 us (38%)
  other arithmetic  25.6 us (5%)
  local copies, waits for them, and re-layouts  23.8 us (5%)
  starting transfers between devices  18.2 us (4%)
    ppermute x9, waiting for transfers between devices, reduce_blocks(): got = lax.ppermute(send, 'dp', swap(bit))  184 us
    pallas_call x1, Pallas kernels, attention(): pl.pallas_call(functools.partial(attention_kernel, head_size), grid=(pair...  66.7 us
    pallas_call x1, Pallas kernels, ffn_forward(): pl.pallas_call(functools.partial(ffn_kernel, rows), grid_spec=pltpu.Prefe...  32.1 us
    pallas_call x1, Pallas kernels, sum_small(): pl.pallas_call(functools.partial(sums_kernel, bits), in_specs=[pl.BlockSp...  22.1 us
    pallas_call x1, Pallas kernels, qkv_forward(): pl.pallas_call(functools.partial(qkv_kernel, tiles), grid_spec=pltpu.Pref...  20.4 us
    pallas_call x1, Pallas kernels, input_gradient(): pl.pallas_call(functools.partial(input_kernel, per_row), grid_spec=pltpu....  19.7 us
    pallas_call x1, Pallas kernels, layer_output(): pl.pallas_call(functools.partial(out_kernel, per_row), grid_spec=pltpu.Pr...  19 us
    pallas_call x1, Pallas kernels, late_grad(): pl.pallas_call(functools.partial(late_grad_kernel, tiles), grid_spec=pltp...  17.6 us
  transfers between devices with their start and end apart: 19, of which 8 were waited for; matrix products, arithmetic and copies ran while one was open for 8% of the time, Pallas kernels for 48%

profile of v1, /device:TPU:0, one launch (start us, length us, event | category | flops | bytes accessed | tf_op | source)
XLA Modules:
  0.0 504.0 jit_solution(16594109203405647237)
XLA Ops:
  0.7 2.8 dynamic-slice_bitcast_fusion.4
  3.5 3.0 collective-permute-start
  6.5 1.1 dynamic-slice_bitcast_fusion.2
  8.4 0.6 reshape.236.gain
  9.0 0.6 reshape.237.bias
  9.6 0.6 reshape.238.bup
  10.2 0.6 pad_add_fusion.1.ids
  11.4 32.1 %ffn_forward.1 = (bf16[1024,1024]{1,0:T(8,128)(2,1)}, bf16[1024,4096]{1,0:T(8,128)(2,1)}, bf16[1024,4096]{1,0:T(8,128)(2,1)}, f32[1,4096]{1,0:T(1,128)}, f32[1,1024]{1,0:T(1,128)}) custom-call(s32[3]{0:T(128)} %pad_add_fusion.1.ids, bf16[1024,1024]{1,0:T(8,128)(2,1)} %bitcast.75, bf16[1024,1024]{1,0:T(8,128)(2,1)} %bitcast.72, bf16[64,1024]{1,0:T(8,128)(2,1)} %fam.7, ...), custom_call_target="tpu_custom_call" | custom-call | flops 17179869184 | bytes 33554432 | tf_op jit(solution)/shard_map/ffn_forward/pallas_call | solution.py:382
  43.4 15.7 %up_grad.1 = (bf16[8,2,32,4096]{3,2,1,0:T(8,128)(2,1)}, bf16[8,2,32,4096]{3,2,1,0:T(8,128)(2,1)}) custom-call(s32[10]{0:T(128)} %pad_add_fusion.3.meta, bf16[1024,1024]{1,0:T(8,128)(2,1)} %get-tuple-element.56.left, bf16[1024,4096]{1,0:T(8,128)(2,1)} %get-tuple-element.41.pre.right), custom_call_target="tpu_custom_call" | custom-call | flops 8589934592 | bytes 18874368 | tf_op jit(solution)/shard_map/up_grad/pallas_call | solution.py:614
  59.1 15.2 %down_grad.1 = (bf16[8,2,128,1024]{3,2,1,0:T(8,128)(2,1)}, bf16[8,2,128,1024]{3,2,1,0:T(8,128)(2,1)}) custom-call(s32[10]{0:T(128)} %pad_add_fusion.3.meta, bf16[1024,4096]{1,0:T(8,128)(2,1)} %get-tuple-element.37.act.left, bf16[1024,1024]{1,0:T(8,128)(2,1)} %bitcast.73), custom_call_target="tpu_custom_call" | custom-call | flops 8589934592 | bytes 18874368 | tf_op jit(solution)/shard_map/down_grad/pallas_call | solution.py:641
  74.8 0.6 reshape.240.bdn
  76.7 1.2 pad_add_fusion.2.ids
  78.0 3.1 fusion.8
  81.1 1.0 copy-done.12
  82.1 20.4 %qkv_forward.1 = (bf16[1024,1024]{1,0:T(8,128)(2,1)}, bf16[1024,1024]{1,0:T(8,128)(2,1)}, bf16[1024,3072]{1,0:T(8,128)(2,1)}, bf16[1024,1024]{1,0:T(8,128)(2,1)}) custom-call(s32[3]{0:T(128)} %pad_add_fusion.2.ids, bf16[512,1024]{1,0:T(8,128)(2,1)} %get-tuple-element.89.own, bf16[512,1024]{1,0:T(8,128)(2,1)} %copy-done.12, ...), custom_call_target="tpu_custom_call" | custom-call | flops 8589934592 | bytes 27262976 | tf_op jit(solution)/shard_map/qkv_forward/pallas_call | solution.py:476
  102.4 66.7 %attention.1 = (bf16[1024,1024]{1,0:T(8,128)(2,1)}, bf16[1024,1024]{1,0:T(8,128)(2,1)}, bf16[1024,1024]{1,0:T(8,128)(2,1)}, bf16[1024,1024]{1,0:T(8,128)(2,1)}) custom-call(bf16[1024,3072]{1,0:T(8,128)(2,1)} %get-tuple-element.38.q_ref.k_ref.v_ref, bf16[1024,3072]{1,0:T(8,128)(2,1)} %get-tuple-element.38.q_ref.k_ref.v_ref, ...), custom_call_target="tpu_custom_call" | custom-call | flops 25769803776 | bytes 16777216 | tf_op jit(solution)/shard_map/attention/pallas_call | solution.py:564
  169.1 12.0 %project_back.1.own = bf16[1024,1024]{1,0:T(8,128)(2,1)} custom-call(bf16[1024,1024]{1,0:T(8,128)(2,1)} %get-tuple-element.42.dq, bf16[1024,1024]{1,0:T(8,128)(2,1)} %get-tuple-element.43.dk, bf16[1024,1024]{1,0:T(8,128)(2,1)} %get-tuple-element.44.dv, bf16[1024,3072]{1,0:T(8,128)(2,1)} %w.1), custom_call_target="tpu_custom_call" | custom-call | flops 6442450944 | bytes 14680064 | tf_op jit(solution)/shard_map/project_back/pallas_call | solution.py:733
  181.1 1.4 dynamic-slice_bitcast_fusion
  182.6 2.1 collective-permute-start.3
  184.6 0.6 pad_add_fusion.ids
  185.4 17.6 %late_grad.1 = (bf16[8,2,32,4096]{3,2,1,0:T(8,128)(2,1)}, bf16[8,2,32,4096]{3,2,1,0:T(8,128)(2,1)}) custom-call(s32[10]{0:T(128)} %pad_add_fusion.3.meta, bf16[1024,1024]{1,0:T(8,128)(2,1)} %get-tuple-element.40.own.att, bf16[1024,1024]{1,0:T(8,128)(2,1)} %get-tuple-element.52.cot, bf16[1024,1024]{1,0:T(8,128)(2,1)} %get-tuple-element.53.norm, ...), custom_call_target="tpu_custom_call" | custom-call | flops 8589934592 | bytes 20971520 | tf_op jit(solution)/shard_map/late_grad/pallas_call | solution.py:687
  203.0 5.8 %collective-permute-done.3.far = bf16[512,1024]{1,0:T(8,128)(2,1)} collective-permute-done((bf16[512,1024]{1,0:T(8,128)(2,1)S(1)}, bf16[512,1024]{1,0:T(8,128)(2,1)}, u32[]{:S(2)}, u32[]{:S(2)}) %collective-permute-start.3) | collective-permute-done | bytes 1048608 | tf_op jit(solution)/shard_map/ppermute | solution.py:1001
  208.7 19.7 %input_gradient.1 = (f32[1024,1024]{1,0:T(8,128)}, f32[1,1024]{1,0:T(1,128)}, f32[1,1024]{1,0:T(1,128)}, f32[2,1024]{1,0:T(2,128)}) custom-call(s32[4]{0:T(128)} %pad_add_fusion.ids, bf16[1024,1024]{1,0:T(8,128)(2,1)} %bitcast.76, bf16[64,1024]{1,0:T(8,128)(2,1)} %fam.7, bf16[2,1024]{1,0:T(2,128)(2,1)} %ori.7, ...), custom_call_target="tpu_custom_call" | custom-call | flops 8589934592 | bytes 29360128 | tf_op jit(solution)/shard_map/input_gradient/pallas_call | solution.py:825
  228.4 2.8 rev.3
  231.2 0.8 slice_add_fusion
  232.0 0.7 constant_dynamic-update-slice_fusion.2
  232.7 0.6 concatenate.18.vec_ref
  233.3 0.7 constant_dynamic-update-slice_fusion.1
  234.0 0.6 copy-done.4
  234.6 22.1 %sum_small.1 = (f32[72,128]{1,0:T(8,128)}, f32[16,16,128]{2,1,0:T(8,128)}) custom-call(f32[72,128]{1,0:T(8,128)} %copy-done.4, f32[16,128]{1,0:T(8,128)} %concatenate.18.vec_ref), custom_call_target="tpu_custom_call" | custom-call | tf_op jit(solution)/shard_map/sum_small/pallas_call | solution.py:900
  256.8 1.3 slice_bitcast_fusion
  258.1 1.3 slice_bitcast_fusion.1
  259.4 0.7 slice.258
  260.1 0.8 slice.257
  260.9 0.6 reshape.250
  261.6 1.2 convert_reduce_fusion
  262.8 1.0 fusion.12
  263.7 1.0 copy-done.13
  264.7 19.0 %layer_output.1 = bf16[1024,1024]{1,0:T(8,128)(2,1)} custom-call(s32[4]{0:T(128)} %pad_add_fusion.ids, bf16[1024,1024]{1,0:T(8,128)(2,1)} %bitcast.77, bf16[64,1024]{1,0:T(8,128)(2,1)} %fam.7, bf16[2,1024]{1,0:T(2,128)(2,1)} %ori.7, bf16[1024,4096]{1,0:T(8,128)(2,1)} %get-tuple-element.37.act.left, bf16[4096,1024]{1,0:T(8,128)(2,1)} %wdn.3, ...), custom_call_target="tpu_custom_call" | custom-call | flops 10737418240 | bytes 27262976 | tf_op jit(solution)/shard_map/layer_output/pallas_call | solution.py:795
  283.7 4.8 add_convert_fusion.3
  288.5 1.2 collective-permute-start.10
  289.7 3.6 add_convert_fusion.1
  293.7 0.9 collective-permute-start.15
  294.6 1.1 copy-done.1
  295.7 3.2 add_convert_fusion.5
  298.9 0.9 collective-permute-start.5
  300.1 37.1 %collective-permute-done.10 = bf16[8,32,4096]{2,1,0:T(8,128)(2,1)S(1)} collective-permute-done((bf16[8,32,4096]{2,1,0:T(8,128)(2,1)S(1)}, bf16[8,32,4096]{2,1,0:T(8,128)(2,1)S(1)}, u32[]{:S(2)}, u32[]{:S(2)}) %collective-permute-start.10) | collective-permute-done | bytes 2097184 | tf_op jit(solution)/shard_map/ppermute | solution.py:715
  337.1 0.9 fusion.3
  338.2 43.8 %collective-permute-done.15 = bf16[8,128,1024]{2,1,0:T(8,128)(2,1)S(1)} collective-permute-done((bf16[8,128,1024]{2,1,0:T(8,128)(2,1)S(1)}, bf16[8,128,1024]{2,1,0:T(8,128)(2,1)S(1)}, u32[]{:S(2)}, u32[]{:S(2)}) %collective-permute-start.15) | collective-permute-done | bytes 2097184 | tf_op jit(solution)/shard_map/ppermute | solution.py:715
  382.1 1.1 fusion.1
  383.3 41.7 %collective-permute-done.5 = bf16[8,32,4096]{2,1,0:T(8,128)(2,1)S(1)} collective-permute-done((bf16[8,32,4096]{2,1,0:T(8,128)(2,1)S(1)}, bf16[8,32,4096]{2,1,0:T(8,128)(2,1)S(1)}, u32[]{:S(2)}, u32[]{:S(2)}) %collective-permute-start.5) | collective-permute-done | bytes 2097184 | tf_op jit(solution)/shard_map/ppermute | solution.py:715
  425.0 0.9 fusion.5
  426.8 3.0 collective-permute-start.17
  429.8 39.3 %collective-permute-done.6 = bf16[4,32,4096]{2,1,0:T(8,128)(2,1)S(1)} collective-permute-done((bf16[4,32,4096]{2,1,0:T(8,128)(2,1)S(1)}, bf16[4,32,4096]{2,1,0:T(8,128)(2,1)S(1)}, u32[]{:S(2)}, u32[]{:S(2)}) %collective-permute-start.6) | collective-permute-done | bytes 1048608 | tf_op jit(solution)/shard_map/ppermute | solution.py:715
  469.5 1.7 collective-permute-start.13
  471.1 15.5 %collective-permute-done.17 = bf16[2,128,1024]{2,1,0:T(8,128)(2,1)S(1)} collective-permute-done((bf16[2,128,1024]{2,1,0:T(8,128)(2,1)S(1)}, bf16[2,128,1024]{2,1,0:T(8,128)(2,1)S(1)}, u32[]{:S(2)}, u32[]{:S(2)}) %collective-permute-start.17) | collective-permute-done | bytes 524320 | tf_op jit(solution)/shard_map/ppermute | solution.py:715
  486.7 2.2 collective-permute-start.18
  488.9 6.6 %collective-permute-done.7 = bf16[2,32,4096]{2,1,0:T(8,128)(2,1)S(1)} collective-permute-done((bf16[2,32,4096]{2,1,0:T(8,128)(2,1)S(1)}, bf16[2,32,4096]{2,1,0:T(8,128)(2,1)S(1)}, u32[]{:S(2)}, u32[]{:S(2)}) %collective-permute-start.7) | collective-permute-done | bytes 524320 | tf_op jit(solution)/shard_map/ppermute | solution.py:715
  495.6 2.0 collective-permute-start.8
  497.6 0.9 bitcast_add_fusion.1
  498.4 0.9 bitcast_add_fusion
  499.3 2.7 collective-permute-done.8
  502.1 0.7 slice.274
  502.8 0.8 slice.273
  (67 shorter events, 4.3 us)
Async XLA Ops:
  0.6 5.9 %copy-start.2 = (bf16[2,512,1024]{2,1,0:T(8,128)(2,1)S(1)}, bf16[2,512,1024]{2,1,0:T(8,128)(2,1)}, u32[]{:S(2)}) copy-start(bf16[2,512,1024]{2,1,0:T(8,128)(2,1)} %param.27) | copy-start | bytes 6291460
  3.5 4.9 copy-start.9
  3.5 5.5 %copy-start.10 = (bf16[1024]{0:T(1024)(128)(2,1)S(1)}, bf16[1024]{0:T(1024)(128)(2,1)}, u32[]{:S(2)}) copy-start(bf16[1024]{0:T(1024)(128)(2,1)} %param.18) | copy-start | bytes 6148
  3.5 6.1 %copy-start.6 = (bf16[4096]{0:T(1024)(128)(2,1)S(1)}, bf16[4096]{0:T(1024)(128)(2,1)}, u32[]{:S(2)}) copy-start(bf16[4096]{0:T(1024)(128)(2,1)} %param.22) | copy-start | bytes 24580
  3.5 6.7 %copy-start.7 = (s32[2]{0:T(128)S(1)}, s32[2]{0:T(128)}, u32[]{:S(2)}) copy-start(s32[2]{0:T(128)} %param.16) | copy-start | bytes 28
  3.5 77.6 %collective-permute-start = (bf16[512,1024]{1,0:T(8,128)(2,1)S(1)}, bf16[512,1024]{1,0:T(8,128)(2,1)S(1)}, u32[]{:S(2)}, u32[]{:S(2)}) collective-permute-start(bf16[512,1024]{1,0:T(8,128)(2,1)S(1)} %get-tuple-element.88), channel_id=1, source_target_pairs={{0,1},{1,0},{2,3},{3,2},{4,5},{5,4},{6,7},{7,6},{8,9},{9,8},{10,11... | collective-permute-start | bytes 3145736 | tf_op jit(solution)/shard_map/ppermute | solution.py:955
  7.7 73.4 %collective-permute-start.1 = (bf16[512,1024]{1,0:T(8,128)(2,1)S(1)}, bf16[512,1024]{1,0:T(8,128)(2,1)}, u32[]{:S(2)}, u32[]{:S(2)}) collective-permute-start(bf16[512,1024]{1,0:T(8,128)(2,1)S(1)} %get-tuple-element.86), channel_id=1, source_target_pairs={{0,1},{1,0},{2,3},{3,2},{4,5},{5,4},{6,7},{7,6},{8,9},{9,8},{10,11... | collective-permute-start | bytes 3145736 | tf_op jit(solution)/shard_map/ppermute | solution.py:956
  59.1 224.6 %collective-permute-start.9 = (bf16[8,2,32,4096]{3,2,1,0:T(8,128)(2,1)}, bf16[8,2,32,4096]{3,2,1,0:T(8,128)(2,1)}, u32[]{:S(2)}, u32[]{:S(2)}) collective-permute-start(bf16[8,2,32,4096]{3,2,1,0:T(8,128)(2,1)} %get-tuple-element.58), channel_id=1, source_target_pairs={{0,2},{2,0},{4,6},{6,4},{8,10},{10,8},{12,14},{14,12},{16,18},{18,... | collective-permute-start | bytes 12582920 | tf_op jit(solution)/shard_map/ppermute | solution.py:710
  59.1 15.7 %copy-start.11 = (bf16[1024]{0:T(1024)(128)(2,1)S(1)}, bf16[1024]{0:T(1024)(128)(2,1)}, u32[]{:S(2)}) copy-start(bf16[1024]{0:T(1024)(128)(2,1)} %param.24) | copy-start | bytes 6148
  59.1 18.8 %copy-start.5 = (f32[1,4096]{1,0:T(1,128)S(1)}, f32[1,4096]{1,0:T(1,128)}, u32[]{:S(2)}) copy-start(f32[1,4096]{1,0:T(1,128)} %get-tuple-element.46) | copy-start | bytes 49156
  59.1 18.8 %copy-start.8 = (f32[1,1024]{1,0:T(1,128)S(1)}, f32[1,1024]{1,0:T(1,128)}, u32[]{:S(2)}) copy-start(f32[1,1024]{1,0:T(1,128)} %get-tuple-element.47) | copy-start | bytes 12292
  74.4 215.4 %collective-permute-start.14 = (bf16[8,2,128,1024]{3,2,1,0:T(8,128)(2,1)}, bf16[8,2,128,1024]{3,2,1,0:T(8,128)(2,1)}, u32[]{:S(2)}, u32[]{:S(2)}) collective-permute-start(bf16[8,2,128,1024]{3,2,1,0:T(8,128)(2,1)} %get-tuple-element.60), channel_id=1, source_target_pairs={{0,2},{2,0},{4,6},{6,4},{8,10},{10,8},{12,14},{14,12},{16,18},{18,... | collective-permute-start | bytes 12582920 | tf_op jit(solution)/shard_map/ppermute | solution.py:710
  81.1 1.0 copy-start.12
  181.1 4.1 copy-start.3
  182.6 26.1 %collective-permute-start.3 = (bf16[512,1024]{1,0:T(8,128)(2,1)S(1)}, bf16[512,1024]{1,0:T(8,128)(2,1)}, u32[]{:S(2)}, u32[]{:S(2)}) collective-permute-start(bf16[512,1024]{1,0:T(8,128)(2,1)S(1)} %dynamic-slice_bitcast_fusion), channel_id=1, source_target_pairs={{0,1},{1,0},{2,3},{3,2},{4,5},{5,4},{6,7},{7,6},{8,9},{9,8},{10,11... | collective-permute-start | bytes 3145736 | tf_op jit(solution)/shard_map/ppermute | solution.py:1001
  185.3 78.4 %collective-permute-start.2 = (bf16[512,1024]{1,0:T(8,128)(2,1)S(1)}, bf16[512,1024]{1,0:T(8,128)(2,1)S(1)}, u32[]{:S(2)}, u32[]{:S(2)}) collective-permute-start(bf16[512,1024]{1,0:T(8,128)(2,1)S(1)} %dynamic-slice_bitcast_fusion.1), channel_id=1, source_target_pairs={{0,1},{1,0},{2,3},{3,2},{4,5},{5,4},{6,7},{7,6},{8,9},{9,8},{10,11... | collective-permute-start | bytes 3145736 | tf_op jit(solution)/shard_map/ppermute | solution.py:999
  203.0 91.7 %collective-permute-start.4 = (bf16[8,2,32,4096]{3,2,1,0:T(8,128)(2,1)}, bf16[8,2,32,4096]{3,2,1,0:T(8,128)(2,1)}, u32[]{:S(2)}, u32[]{:S(2)}) collective-permute-start(bf16[8,2,32,4096]{3,2,1,0:T(8,128)(2,1)} %get-tuple-element.55), channel_id=1, source_target_pairs={{0,2},{2,0},{4,6},{6,4},{8,10},{10,8},{12,14},{14,12},{16,18},{18,... | collective-permute-start | bytes 12582920 | tf_op jit(solution)/shard_map/ppermute | solution.py:710
  234.0 0.6 copy-start.4
  263.7 1.0 copy-start.13
  283.7 6.0 %copy-start = (bf16[8,2,128,1024]{3,2,1,0:T(8,128)(2,1)S(1)}, bf16[8,2,128,1024]{3,2,1,0:T(8,128)(2,1)}, u32[]{:S(2)}) copy-start(bf16[8,2,128,1024]{3,2,1,0:T(8,128)(2,1)} %get-tuple-element.59) | copy-start | bytes 12582916
  288.5 48.6 %collective-permute-start.10 = (bf16[8,32,4096]{2,1,0:T(8,128)(2,1)S(1)}, bf16[8,32,4096]{2,1,0:T(8,128)(2,1)S(1)}, u32[]{:S(2)}, u32[]{:S(2)}) collective-permute-start(bf16[8,32,4096]{2,1,0:T(8,128)(2,1)S(1)} %bitcast.79), channel_id=1, source_target_pairs={{0,4},{2,6},{4,0},{6,2},{8,12},{10,14},{12,8},{14,10},{16,20},{18,... | collective-permute-start | bytes 6291464 | tf_op jit(solution)/shard_map/ppermute | solution.py:715
  293.5 2.2 copy-start.1
  293.7 88.3 %collective-permute-start.15 = (bf16[8,128,1024]{2,1,0:T(8,128)(2,1)S(1)}, bf16[8,128,1024]{2,1,0:T(8,128)(2,1)S(1)}, u32[]{:S(2)}, u32[]{:S(2)}) collective-permute-start(bf16[8,128,1024]{2,1,0:T(8,128)(2,1)S(1)} %bitcast.78), channel_id=1, source_target_pairs={{0,4},{2,6},{4,0},{6,2},{8,12},{10,14},{12,8},{14,10},{16,20},{18,... | collective-permute-start | bytes 6291464 | tf_op jit(solution)/shard_map/ppermute | solution.py:715
  298.9 126.1 %collective-permute-start.5 = (bf16[8,32,4096]{2,1,0:T(8,128)(2,1)S(1)}, bf16[8,32,4096]{2,1,0:T(8,128)(2,1)S(1)}, u32[]{:S(2)}, u32[]{:S(2)}) collective-permute-start(bf16[8,32,4096]{2,1,0:T(8,128)(2,1)S(1)} %bitcast.80), channel_id=1, source_target_pairs={{0,4},{2,6},{4,0},{6,2},{8,12},{10,14},{12,8},{14,10},{16,20},{18,... | collective-permute-start | bytes 6291464 | tf_op jit(solution)/shard_map/ppermute | solution.py:715
  338.0 88.0 %collective-permute-start.11 = (bf16[4,32,4096]{2,1,0:T(8,128)(2,1)S(1)}, bf16[4,32,4096]{2,1,0:T(8,128)(2,1)S(1)}, u32[]{:S(2)}, u32[]{:S(2)}) collective-permute-start(bf16[4,32,4096]{2,1,0:T(8,128)(2,1)S(1)} %get-tuple-element.77), channel_id=1, source_target_pairs={{0,8},{2,10},{4,12},{6,14},{8,0},{10,2},{12,4},{14,6},{16,24},{18,... | collective-permute-start | bytes 3145736 | tf_op jit(solution)/shard_map/ppermute | solution.py:715
  383.2 43.2 %collective-permute-start.16 = (bf16[4,128,1024]{2,1,0:T(8,128)(2,1)S(1)}, bf16[4,128,1024]{2,1,0:T(8,128)(2,1)S(1)}, u32[]{:S(2)}, u32[]{:S(2)}) collective-permute-start(bf16[4,128,1024]{2,1,0:T(8,128)(2,1)S(1)} %get-tuple-element.71), channel_id=1, source_target_pairs={{0,8},{2,10},{4,12},{6,14},{8,0},{10,2},{12,4},{14,6},{16,24},{18,... | collective-permute-start | bytes 3145736 | tf_op jit(solution)/shard_map/ppermute | solution.py:715
  426.0 43.1 %collective-permute-start.6 = (bf16[4,32,4096]{2,1,0:T(8,128)(2,1)S(1)}, bf16[4,32,4096]{2,1,0:T(8,128)(2,1)S(1)}, u32[]{:S(2)}, u32[]{:S(2)}) collective-permute-start(bf16[4,32,4096]{2,1,0:T(8,128)(2,1)S(1)} %get-tuple-element.83), channel_id=1, source_target_pairs={{0,8},{2,10},{4,12},{6,14},{8,0},{10,2},{12,4},{14,6},{16,24},{18,... | collective-permute-start | bytes 3145736 | tf_op jit(solution)/shard_map/ppermute | solution.py:715
  426.3 43.1 %collective-permute-start.12 = (bf16[2,32,4096]{2,1,0:T(8,128)(2,1)S(1)}, bf16[2,32,4096]{2,1,0:T(8,128)(2,1)S(1)}, u32[]{:S(2)}, u32[]{:S(2)}) collective-permute-start(bf16[2,32,4096]{2,1,0:T(8,128)(2,1)S(1)} %get-tuple-element.75), channel_id=1, source_target_pairs={{0,16},{2,18},{4,20},{6,22},{8,24},{10,26},{12,28},{14,30},{16,0},... | collective-permute-start | bytes 1572872 | tf_op jit(solution)/shard_map/ppermute | solution.py:715
  426.8 59.9 %collective-permute-start.17 = (bf16[2,128,1024]{2,1,0:T(8,128)(2,1)S(1)}, bf16[2,128,1024]{2,1,0:T(8,128)(2,1)S(1)}, u32[]{:S(2)}, u32[]{:S(2)}) collective-permute-start(bf16[2,128,1024]{2,1,0:T(8,128)(2,1)S(1)} %get-tuple-element.69), channel_id=1, source_target_pairs={{0,16},{2,18},{4,20},{6,22},{8,24},{10,26},{12,28},{14,30},{16,0},... | collective-permute-start | bytes 1572872 | tf_op jit(solution)/shard_map/ppermute | solution.py:715
  469.3 26.2 %collective-permute-start.7 = (bf16[2,32,4096]{2,1,0:T(8,128)(2,1)S(1)}, bf16[2,32,4096]{2,1,0:T(8,128)(2,1)S(1)}, u32[]{:S(2)}, u32[]{:S(2)}) collective-permute-start(bf16[2,32,4096]{2,1,0:T(8,128)(2,1)S(1)} %get-tuple-element.81), channel_id=1, source_target_pairs={{0,16},{2,18},{4,20},{6,22},{8,24},{10,26},{12,28},{14,30},{16,0},... | collective-permute-start | bytes 1572872 | tf_op jit(solution)/shard_map/ppermute | solution.py:715
  469.5 28.1 %collective-permute-start.13 = (bf16[32,4096]{1,0:T(8,128)(2,1)S(1)}, bf16[32,4096]{1,0:T(8,128)(2,1)S(1)}, u32[]{:S(2)}, u32[]{:S(2)}) collective-permute-start(bf16[32,4096]{1,0:T(8,128)(2,1)S(1)} %fusion.10), channel_id=1, source_target_pairs={{0,1},{1,0},{2,3},{3,2},{4,5},{5,4},{6,7},{7,6},{8,9},{9,8},{10,11... | collective-permute-start | bytes 786440 | tf_op jit(solution)/shard_map/ppermute | solution.py:718
  486.7 11.7 %collective-permute-start.18 = (bf16[128,1024]{1,0:T(8,128)(2,1)S(1)}, bf16[128,1024]{1,0:T(8,128)(2,1)S(1)}, u32[]{:S(2)}, u32[]{:S(2)}) collective-permute-start(bf16[128,1024]{1,0:T(8,128)(2,1)S(1)} %fusion.11), channel_id=1, source_target_pairs={{0,1},{1,0},{2,3},{3,2},{4,5},{5,4},{6,7},{7,6},{8,9},{9,8},{10,11... | collective-permute-start | bytes 786440 | tf_op jit(solution)/shard_map/ppermute | solution.py:718
  495.6 6.4 %collective-permute-start.8 = (bf16[32,4096]{1,0:T(8,128)(2,1)S(1)}, bf16[32,4096]{1,0:T(8,128)(2,1)S(1)}, u32[]{:S(2)}, u32[]{:S(2)}) collective-permute-start(bf16[32,4096]{1,0:T(8,128)(2,1)S(1)} %fusion.9), channel_id=1, source_target_pairs={{0,1},{1,0},{2,3},{3,2},{4,5},{5,4},{6,7},{7,6},{8,9},{9,8},{10,11... | collective-permute-start | bytes 786440 | tf_op jit(solution)/shard_map/ppermute | solution.py:718
